TPU v7x, 32 devices: a whole 2x2x4 slice. The times are simulated.
32 devices in a mesh: dp: 16 (over z, x, core), seq: 2 (over y).
Axes of the slice: x: 2, y: 2, z: 4, core: 2. Of those that a mesh axis runs over, the one named last changes fastest.
Arguments:
- captions: bfloat16 [16, 1024, 768], P('dp', 'seq'), may hold values from -6 to 6
- patches: bfloat16 [16, 196, 768], P('dp', 'seq'), may hold values from -32 to 32, as said below
- prefix: bfloat16 [16, 32, 768], P('dp', 'seq'), may hold values from -6 to 6
- prefix_count: int32 [16], P('dp'), may hold values from 0 to 32, as said below
- caption_len: int32 [16], P('dp'), may hold values from 513 to 1024, as said below
- cotangent: bfloat16 [16, 1024, 768], P('dp', 'seq'), may hold values from -6 to 6
- w_patch: bfloat16 [768, 768], P('dp'), may hold values from -0.21875 to 0.21875
- w_conv: bfloat16 [2, 6912, 768], P(None, 'dp'), may hold values from -0.078125 to 0.078125
- w_self_qkv: bfloat16 [768, 2304], P('dp'), may hold values from -0.21875 to 0.21875
- w_self_out: bfloat16 [768, 768], P('dp'), may hold values from -3.5 to 3.5
- w_cross_q: bfloat16 [768, 768], P('dp'), may hold values from -0.21875 to 0.21875
- w_cross_kv: bfloat16 [768, 1536], P('dp'), may hold values from -0.21875 to 0.21875
- w_cross_out: bfloat16 [768, 768], P('dp'), may hold values from -1.75 to 1.75
- w_up: bfloat16 [768, 3072], P('dp'), may hold values from -0.21875 to 0.21875
- w_down: bfloat16 [3072, 768], P('dp'), may hold values from -0.109375 to 0.109375
- norm_params: bfloat16 [12, 768], P(None, 'dp'), may hold values from 0.25 to 1.75
Outputs:
- block_output: bfloat16 [16, 1024, 768], P('dp', 'seq')
- caption_grad: bfloat16 [16, 1024, 768], P('dp', 'seq')
- prefix_grad: bfloat16 [16, 32, 768], P('dp', 'seq')
- grad_w_patch: float32 [768, 768], P('dp')
- grad_w_conv: float32 [2, 6912, 768], P(None, 'dp')
- grad_w_self_qkv: float32 [768, 2304], P('dp')
- grad_w_self_out: float32 [768, 768], P('dp')
- grad_w_cross_q: float32 [768, 768], P('dp')
- grad_w_cross_kv: float32 [768, 1536], P('dp')
- grad_w_cross_out: float32 [768, 768], P('dp')
- grad_w_up: float32 [768, 3072], P('dp')
- grad_w_down: float32 [3072, 768], P('dp')
- grad_norm_params: float32 [12, 768], P(None, 'dp')
Inputs may be any that keep to these rules, and one draw needn't show every extreme that they name: `prefix_count`: each example has between 0 and 32 live prefix slots; some example has all 32 and some none. `caption_len`: every caption reaches past the first 512 slots; some caption fills all 1024 slots. `patches`: pixel values; each example has its own overall scale.
All inputs are finite; a program needn't handle non-finite values.
Results may differ from a plain program's by a relative error of at most 0.035.
Values may be sent and summed in bfloat16 or wider, within the bound.
A program may use at most 384 MiB of HBM per device.

v0:
```python
import functools

import jax
import jax.numpy as jnp
import numpy as np
from jax import lax
from jax.experimental import pallas as pl
from jax.experimental.pallas import tpu as pltpu
from jax.sharding import PartitionSpec as P

HEADS = 12
SIDE = 14
MESH = pl.DeviceIdType.MESH
LOW = jnp.bfloat16

STEPS = ((4, 3, 2, 0), (4, 0, 3, 2), (4, 2, 0, 3))
PORTIONS = 3
GROUP = 8


def my_bits():
    a = lax.axis_index("dp")
    return [
        lax.axis_index("seq"),
        lax.rem(a, 2),
        lax.rem(a // 2, 2),
        lax.rem(a // 4, 2),
        lax.rem(a // 8, 2),
    ]


def flipped(bits, which):
    return [1 - b if i == which else b for i, b in enumerate(bits)]


def place(bits):
    return (bits[1] + 2 * bits[2] + 4 * bits[3] + 8 * bits[4], bits[0])


def slot_of(bits, p):
    order = STEPS[p]
    return (
        bits[order[0]] + 2 * bits[order[1]] + 4 * bits[order[2]] + 8 * bits[order[3]] + 16 * bits[1]
    )


def device_of_slot(p):
    owners = np.zeros(32, np.int64)
    for e in range(32):
        bits = [(e >> i) & 1 for i in range(5)]
        owners[int(slot_of(bits, p))] = e
    return owners


def slots_to_devices(array):
    parts = []
    for p in range(PORTIONS):
        rest = array.shape[2:]
        names = [1, STEPS[p][3], STEPS[p][2], STEPS[p][1], STEPS[p][0]]
        cube = array[p].reshape((2,) * 5 + rest)
        perm = [names.index(bit) for bit in (4, 3, 2, 1, 0)]
        cube = cube.transpose(perm + [5 + i for i in range(len(rest))])
        parts.append(cube.reshape((32,) + rest))
    return jnp.stack(parts, 1)


def devices_to_slots(array):
    parts = []
    for p in range(PORTIONS):
        rest = array.shape[2:]
        names = [4, 3, 2, 1, 0]
        cube = array[:, p].reshape((2,) * 5 + rest)
        want = [1, STEPS[p][3], STEPS[p][2], STEPS[p][1], STEPS[p][0]]
        perm = [names.index(bit) for bit in want]
        cube = cube.transpose(perm + [5 + i for i in range(len(rest))])
        parts.append(cube.reshape((32,) + rest))
    return jnp.stack(parts, 0)


def greet(places):
    barrier = pltpu.get_barrier_semaphore()
    for where in places:
        pl.semaphore_signal(barrier, inc=1, device_id=where, device_id_type=MESH)
    pl.semaphore_wait(barrier, len(places))


def arrived(ref, sem):
    pltpu.make_async_remote_copy(
        src_ref=ref,
        dst_ref=ref,
        send_sem=sem,
        recv_sem=sem,
        device_id=(lax.axis_index("dp"), 1 - lax.axis_index("seq")),
        device_id_type=MESH,
    ).wait_recv()


def with_mask(bits, mask):
    return [1 - b if (mask >> i) & 1 else b for i, b in enumerate(bits)]


def number_of(bits):
    return bits[0] + 2 * bits[1] + 4 * bits[2] + 8 * bits[3] + 16 * bits[4]


def stem_part(ref, bits, p):
    return ref.at[p, pl.ds(slot_of(bits, p), 1)]


def stem_own(ref, bits, p):
    return ref.at[pl.ds(p, 1)]


def rows_part(ref, bits, p):
    width = ref.shape[2] // PORTIONS
    return ref.at[number_of(bits), :, pl.ds(p * width, width)]


def rows_own(ref, bits, p):
    width = ref.shape[1] // PORTIONS
    return ref.at[:, pl.ds(p * width, width)]


KINDS = {
    "stem": (stem_own, stem_part),
    "rows": (rows_own, rows_part),
}


def gather_steps(kinds, swaps, pairs, refs):
    count = len(kinds)
    total = count + swaps + pairs
    ins, outs, sems = refs[:total], refs[total : 2 * total], refs[2 * total :]
    send_sem, recv_sem, own_sem, swap_send, swap_recv, pair_send, pair_recv = sems
    bits = my_bits()
    a, s = lax.axis_index("dp"), bits[0]
    dp = ins[count].shape[0] if swaps else 1
    partners = [place(flipped(bits, b)) for b in range(5)]
    partners += [(lax.rem(a + j, dp), s) for j in range(1, dp)]

    def own_of(i, p):
        return KINDS[kinds[i]][0](ins[i], bits, p)

    def part_of(i, p, mask):
        return KINDS[kinds[i]][1](outs[i], with_mask(bits, mask), p)

    def block(i, p, mask, bit):
        return pltpu.make_async_remote_copy(
            src_ref=own_of(i, p) if mask == 0 else part_of(i, p, mask),
            dst_ref=part_of(i, p, mask),
            send_sem=send_sem.at[i, p, mask ^ (1 << bit)],
            recv_sem=recv_sem.at[i, p, mask ^ (1 << bit)],
            device_id=place(flipped(bits, bit)),
            device_id_type=MESH,
        )

    def await_part(i, p, mask):
        arrived(part_of(i, p, mask), recv_sem.at[i, p, mask])

    def own_copy(i, p):
        return pltpu.make_async_copy(own_of(i, p), part_of(i, p, 0), own_sem.at[i, p])

    def swap_own():
        return pltpu.make_async_copy(ins[count].at[a], outs[count].at[a], swap_send.at[0])

    def swap_copy(j):
        to = lax.rem(a + j, dp)
        return pltpu.make_async_remote_copy(
            src_ref=ins[count].at[to],
            dst_ref=outs[count].at[a],
            send_sem=swap_send.at[j],
            recv_sem=swap_recv.at[j],
            device_id=(to, s),
            device_id_type=MESH,
        )

    def pair_copy(j):
        return pltpu.make_async_remote_copy(
            src_ref=ins[count + swaps + j],
            dst_ref=outs[count + swaps + j],
            send_sem=pair_send.at[j],
            recv_sem=pair_recv.at[j],
            device_id=(a, 1 - s),
            device_id_type=MESH,
        )

    every = [(i, p) for i in range(count) for p in range(PORTIONS)]
    held = {p: [0] for p in range(PORTIONS)}
    fresh = {p: [0] for p in range(PORTIONS)}
    sent = []
    steps = []
    for k in range(5):
        plan = []
        for i in range(count):
            for p in range(PORTIONS):
                waits = list(fresh[p]) if k else []
                links = [(mask, STEPS[p][k]) for mask in held[p]] if k < 4 else []
                plan.append((i, p, waits, links))
                sent += [(i, p, mask, bit) for mask, bit in links]
            for p in range(PORTIONS):
                cores = [(mask, 1) for mask in fresh[p]]
                plan.append((i, p, [], cores))
                sent += [(i, p, mask, bit) for mask, bit in cores]

        def run(k=k, plan=plan):
            if k == 0:
                greet(partners)
            for i, p, waits, sends in plan:
                for mask in waits:
                    await_part(i, p, mask)
                for mask, bit in sends:
                    block(i, p, mask, bit).start()
            if k == 0:
                for i, p in every:
                    own_copy(i, p).start()
                for j in range(pairs):
                    pair_copy(j).start()
                if swaps:
                    swap_own().start()
                for j in range(1, dp):
                    swap_copy(j).start()

        steps.append(run)
        if k < 4:
            for p in range(PORTIONS):
                fresh[p] = [mask ^ (1 << STEPS[p][k]) for mask in held[p]]
                held[p] = held[p] + fresh[p]

    def finish():
        for i, p in every:
            for mask in held[p]:
                await_part(i, p, mask ^ 2)
        for j in range(1, dp):
            arrived(outs[count].at[lax.rem(a - j + dp, dp)], swap_recv.at[j])
        for j in range(pairs):
            pair_copy(j).wait()
        for i, p, mask, bit in sent:
            block(i, p, mask, bit).wait_send()
        for j in range(1, dp):
            swap_copy(j).wait_send()
        for i, p in every:
            own_copy(i, p).wait()
        if swaps:
            swap_own().wait()

    steps.append(finish)
    return steps


def gather_body(kinds, swaps, pairs, *refs):
    for step in gather_steps(kinds, swaps, pairs, refs):
        step()


def gather_sems(count, pairs):
    return [
        pltpu.SemaphoreType.DMA((count, PORTIONS, 32)),
        pltpu.SemaphoreType.DMA((count, PORTIONS, 32)),
        pltpu.SemaphoreType.DMA((count, PORTIONS)),
        pltpu.SemaphoreType.DMA((16,)),
        pltpu.SemaphoreType.DMA((16,)),
        pltpu.SemaphoreType.DMA((max(pairs, 1),)),
        pltpu.SemaphoreType.DMA((max(pairs, 1),)),
    ]


def gather_many(stems, rows, swaps, pairs, cid):
    kinds = ["stem"] * len(stems) + ["rows"] * len(rows)
    arrays = list(stems) + list(rows) + list(swaps) + list(pairs)
    shapes = [jax.ShapeDtypeStruct((PORTIONS, 32) + x.shape[1:], x.dtype) for x in stems]
    shapes += [jax.ShapeDtypeStruct((32,) + x.shape, x.dtype) for x in rows]
    shapes += [jax.ShapeDtypeStruct(x.shape, x.dtype) for x in list(swaps) + list(pairs)]
    space = pl.BlockSpec(memory_space=pltpu.HBM)
    return pl.pallas_call(
        functools.partial(gather_body, tuple(kinds), len(swaps), len(pairs)),
        name="gather_many",
        out_shape=tuple(shapes),
        in_specs=[space] * len(arrays),
        out_specs=(space,) * len(arrays),
        scratch_shapes=gather_sems(len(kinds), len(pairs)),
        compiler_params=pltpu.CompilerParams(collective_id=cid, has_side_effects=True),
    )(*arrays)


def attend_gather_body(width, *refs):
    info_ref, ok_ref, q_ref, k_ref, v_ref, x_ref, o_ref, lse_ref, all_ref = refs[:9]
    steps = gather_steps(("stem",), 0, 0, (x_ref, all_ref) + refs[9:])
    for at, step in enumerate(steps[:-1]):

        @pl.when(pl.program_id(0) == at)
        def _():
            step()

    attend_body("self", width, info_ref, ok_ref, q_ref, k_ref, v_ref, o_ref, lse_ref)

    @pl.when(pl.program_id(0) == pl.num_programs(0) - 1)
    def _():
        steps[-1]()


def attend_gather(info, ok, q, k, v, x, cid):
    rows, features = q.shape
    keys = k.shape[0]
    width = features // HEADS
    pairs = features // PAIR
    return pl.pallas_call(
        functools.partial(attend_gather_body, width),
        name="attend_gather",
        grid=(pairs,),
        in_specs=attention_specs(rows, keys, ok) + [pl.BlockSpec(memory_space=pltpu.HBM)],
        out_specs=(
            pl.BlockSpec((rows, PAIR), lambda i: (0, i)),
            pl.BlockSpec((1, 8, rows), lambda i: (i, 0, 0)),
            pl.BlockSpec(memory_space=pltpu.HBM),
        ),
        out_shape=(
            jax.ShapeDtypeStruct((rows, features), LOW),
            jax.ShapeDtypeStruct((pairs, 8, rows), jnp.float32),
            jax.ShapeDtypeStruct((PORTIONS, 32) + x.shape[1:], x.dtype),
        ),
        scratch_shapes=gather_sems(1, 0),
        compiler_params=pltpu.CompilerParams(
            collective_id=cid, has_side_effects=True, vmem_limit_bytes=48 << 20
        ),
    )(info, ok, q, k, v, x)


def pack_body(pieces, *refs):
    ins, o_ref = refs[:-1], refs[-1]
    rows, cols = o_ref.shape[1:]
    for at, (which, row, col) in enumerate(pieces):
        o_ref[at] = ins[which][row : row + rows, col : col + cols]


def pack(pieces, arrays, rows, cols):
    return pl.pallas_call(
        functools.partial(pack_body, tuple(pieces)),
        name="pack",
        out_shape=jax.ShapeDtypeStruct((len(pieces), rows, cols), arrays[0].dtype),
    )(*arrays)


def reduce_body(x_ref, o_ref, r0, r1, r2, r3, r4, send_sem, recv_sem):
    bits = my_bits()
    greet([place(flipped(bits, b)) for b in range(5)])
    started = []
    slots = [slot_of(bits, p) for p in range(PORTIONS)]
    bufs = (r0, r1, r2, r3, r4)

    def send(p, src, dst, bit, k):
        copy = pltpu.make_async_remote_copy(
            src_ref=src,
            dst_ref=dst,
            send_sem=send_sem.at[p, k],
            recv_sem=recv_sem.at[p, k],
            device_id=place(flipped(bits, bit)),
            device_id_type=MESH,
        )
        copy.start()
        started.append(copy)

    for p in range(PORTIONS):
        away = 16 * (1 - bits[1])
        send(p, x_ref.at[p, pl.ds(away, 16)], r0.at[p], 1, 0)
    for k in range(5):
        size = 16 >> k
        for p in range(PORTIONS):
            got = bufs[k].at[p]
            arrived(got, recv_sem.at[p, k])
            if k == 0:
                base, held = 16 * bits[1], x_ref
            else:
                bit = bits[STEPS[p][4 - k]]
                base, held = size * bit, bufs[k - 1]
            if k == 4:
                o_ref[p] = held[p, base].astype(jnp.float32) + bufs[k][p, 0].astype(jnp.float32)
                continue
            for j in range(size):
                total = held[p, base + j].astype(jnp.float32) + bufs[k][p, j].astype(jnp.float32)
                bufs[k][p, j] = total.astype(bufs[k].dtype)
            half = size // 2
            nbit = bits[STEPS[p][3 - k]]
            send(
                p,
                bufs[k].at[p, pl.ds(half * (1 - nbit), half)],
                bufs[k + 1].at[p],
                STEPS[p][3 - k],
                k + 1,
            )
    for copy in started:
        copy.wait_send()


def reduce_all(x, cid):
    rest = x.shape[2:]
    return pl.pallas_call(
        reduce_body,
        name="reduce_all",
        out_shape=jax.ShapeDtypeStruct((PORTIONS,) + rest, jnp.float32),
        in_specs=[pl.BlockSpec(memory_space=pltpu.VMEM)],
        out_specs=pl.BlockSpec(memory_space=pltpu.VMEM),
        scratch_shapes=[pltpu.VMEM((PORTIONS, 16 >> k) + rest, x.dtype) for k in range(5)]
        + [pltpu.SemaphoreType.DMA((PORTIONS, 5)), pltpu.SemaphoreType.DMA((PORTIONS, 5))],
        compiler_params=pltpu.CompilerParams(
            collective_id=cid, has_side_effects=True, vmem_limit_bytes=40 << 20
        ),
    )(x)


def swap_both_body(x_ref, o_ref, send_sem, recv_sem, pass_sem, got_sem, own_sem):
    a, s = lax.axis_index("dp"), lax.axis_index("seq")
    count = x_ref.shape[0]
    greet([(lax.rem(a + j, count), s) for j in range(1, count)] + [(a, 1 - s)])
    own = pltpu.make_async_copy(x_ref.at[a], o_ref.at[s, a], own_sem)
    own.start()
    copies = []

    def pass_on(src, slot, j):
        copy = pltpu.make_async_remote_copy(
            src_ref=src,
            dst_ref=o_ref.at[s, slot],
            send_sem=pass_sem.at[j],
            recv_sem=got_sem.at[j],
            device_id=(a, 1 - s),
            device_id_type=MESH,
        )
        copy.start()
        copies.append(copy)

    pass_on(x_ref.at[a], a, 0)
    for j in range(1, count):
        to = lax.rem(a + j, count)
        copy = pltpu.make_async_remote_copy(
            src_ref=x_ref.at[to],
            dst_ref=o_ref.at[s, a],
            send_sem=send_sem.at[j],
            recv_sem=recv_sem.at[j],
            device_id=(to, s),
            device_id_type=MESH,
        )
        copy.start()
        copies.append(copy)
    for j in range(1, count):
        source = lax.rem(a - j + count, count)
        got = o_ref.at[s, source]
        arrived(got, recv_sem.at[j])
        pass_on(got, source, j)
    for j in range(count):
        got = o_ref.at[1 - s, lax.rem(a - j + count, count)]
        arrived(got, got_sem.at[j])
    for copy in copies:
        copy.wait_send()
    own.wait()


def swap_both(x, cid):
    count = x.shape[0]
    return pl.pallas_call(
        swap_both_body,
        name="swap_both",
        out_shape=jax.ShapeDtypeStruct((2,) + x.shape, x.dtype),
        in_specs=[pl.BlockSpec(memory_space=pltpu.HBM)],
        out_specs=pl.BlockSpec(memory_space=pltpu.HBM),
        scratch_shapes=[pltpu.SemaphoreType.DMA((count,))] * 4 + [pltpu.SemaphoreType.DMA],
        compiler_params=pltpu.CompilerParams(collective_id=cid, has_side_effects=True),
    )(x)


def exchange_body(x_ref, o_ref, send_sem, recv_sem, own_sem):
    e = 2 * lax.axis_index("dp") + lax.axis_index("seq")
    count = x_ref.shape[0]

    def where(number):
        return (number // 2, lax.rem(number, 2))

    greet([where(lax.rem(e + j, count)) for j in range(1, count)])
    own = pltpu.make_async_copy(x_ref.at[e], o_ref.at[e], own_sem)
    own.start()
    copies = []
    for j in range(1, count):
        to = lax.rem(e + j, count)
        copy = pltpu.make_async_remote_copy(
            src_ref=x_ref.at[to],
            dst_ref=o_ref.at[e],
            send_sem=send_sem.at[j],
            recv_sem=recv_sem.at[j],
            device_id=where(to),
            device_id_type=MESH,
        )
        copy.start()
        copies.append(copy)
    for j in range(1, count):
        got = o_ref.at[lax.rem(e - j + count, count)]
        arrived(got, recv_sem.at[j])
    for copy in copies:
        copy.wait_send()
    own.wait()


def exchange_all(x, cid):
    count = x.shape[0]
    return pl.pallas_call(
        exchange_body,
        name="exchange_all",
        out_shape=jax.ShapeDtypeStruct(x.shape, x.dtype),
        in_specs=[pl.BlockSpec(memory_space=pltpu.HBM)],
        out_specs=pl.BlockSpec(memory_space=pltpu.HBM),
        scratch_shapes=[
            pltpu.SemaphoreType.DMA((count,)),
            pltpu.SemaphoreType.DMA((count,)),
            pltpu.SemaphoreType.DMA,
        ],
        compiler_params=pltpu.CompilerParams(collective_id=cid, has_side_effects=True),
    )(x)


GELU_C = 0.7978845608028654
GELU_A = 0.044715


def gelu_of(x):
    return 0.5 * x * (1.0 + jnp.tanh(GELU_C * (x + GELU_A * (x * x * x))))


def gelu_slope(x):
    t = jnp.tanh(GELU_C * (x + GELU_A * (x * x * x)))
    return 0.5 * (1.0 + t) + 0.5 * x * (1.0 - t * t) * (GELU_C * (1.0 + 3.0 * GELU_A * (x * x)))


CHUNK = 640


def tap_masks(cells, examples):
    rows = examples * SIDE * SIDE
    at = np.arange(rows)
    i, j = (at // SIDE) % SIDE, at % SIDE
    out = np.zeros((16, cells), np.float32)
    for r in range(3):
        for c in range(3):
            ok = (i + r - 1 >= 0) & (i + r - 1 < SIDE) & (j + c - 1 >= 0) & (j + c - 1 < SIDE)
            out[3 * r + c, :rows] = ok
    out[9, :rows] = 1.0
    return out


def tap_shift(tap):
    return SIDE * (tap // 3 - 1) + tap % 3 - 1


def norm_act(values, valid, gain, bias, number):
    centre = jnp.sum(values, 1, keepdims=True) / number
    away = jnp.where(valid > 0, values - centre, 0.0)
    rstd = lax.rsqrt(jnp.sum(away * away, 1, keepdims=True) / number + 1e-05)
    normed = away * rstd
    return normed, rstd, gelu_of(normed * gain + bias)


def put_low(x_ref, y):
    for p in range(PORTIONS):
        x_ref[p] = y[GROUP * p : GROUP * (p + 1)].astype(x_ref.dtype)


def first_body(number, p_ref, w_ref, gb_ref, m_ref, n_ref, rstd_ref, y_ref, x_ref, v_ref):
    blocks, size = p_ref.shape[0], p_ref.shape[1]
    v_ref[:, blocks * size :] = jnp.zeros((v_ref.shape[0], v_ref.shape[1] - blocks * size), jnp.float32)
    for block in range(blocks):
        v_ref[:, block * size : (block + 1) * size] = lax.dot_general(
            w_ref[...], p_ref[block], (((1,), (1,)), ((), ())), preferred_element_type=jnp.float32
        )
    normed, rstd, act = norm_act(v_ref[...], m_ref[9:10, :], gb_ref[:, 0:1], gb_ref[:, 1:2], number)
    n_ref[...] = normed
    rstd_ref[...] = jnp.broadcast_to(rstd, rstd_ref.shape)
    y_ref[...] = act
    put_low(x_ref, act)


def conv_body(number, layer, x_in, w_ref, gb_ref, m_ref, y_in, n_ref, rstd_ref, y_ref, x_ref, z_ref):
    cells = x_in.shape[1]
    rows = y_in.shape[0]
    for start in range(0, cells, CHUNK):
        z_ref[:, start : start + CHUNK] = jnp.dot(
            w_ref[...], x_in[:, start : start + CHUNK], preferred_element_type=jnp.float32
        )
    total = jnp.zeros((rows, cells), jnp.float32)
    for tap in range(9):
        moved = z_ref[rows * tap : rows * (tap + 1), :]
        shift = (-tap_shift(tap)) % cells
        if shift:
            moved = pltpu.roll(moved, shift, 1)
        total = total + jnp.where(m_ref[tap : tap + 1, :] > 0, moved, 0.0)
    normed, rstd, act = norm_act(
        total,
        m_ref[9:10, :],
        gb_ref[:, 2 * layer : 2 * layer + 1],
        gb_ref[:, 2 * layer + 1 : 2 * layer + 2],
        number,
    )
    n_ref[...] = normed
    rstd_ref[...] = jnp.broadcast_to(rstd, rstd_ref.shape)
    y = y_in[...] + act
    y_ref[...] = y
    put_low(x_ref, y)


def norm_slope(number, dy, normed, rstd, gain, bias):
    e = dy * gelu_slope(normed * gain + bias)
    d_gain = jnp.sum(e * normed, 1, keepdims=True)
    d_bias = jnp.sum(e, 1, keepdims=True)
    dn = e * gain
    mean_dn = d_bias * gain / number
    mean_dnn = d_gain * gain / number
    return rstd * (dn - mean_dn - normed * mean_dnn), d_gain, d_bias


def conv_back_body(
    number, layer, dy_ref, n_ref, rstd_ref, gb_ref, m_ref, x_in, wt_ref, dx_ref, g_ref, s_ref, d_ref
):
    cells = x_in.shape[1]
    rows = dy_ref.shape[0]
    dv, d_gain, d_bias = norm_slope(
        number,
        dy_ref[...],
        n_ref[...],
        rstd_ref[:, 0:1],
        gb_ref[:, 2 * layer : 2 * layer + 1],
        gb_ref[:, 2 * layer + 1 : 2 * layer + 2],
    )
    lanes = lax.broadcasted_iota(jnp.int32, s_ref.shape, 1)
    s_ref[...] = jnp.where(lanes == 0, d_gain, d_bias)
    for tap in range(9):
        shift = tap_shift(tap) % cells
        moved = pltpu.roll(dv, shift, 1) if shift else dv
        moved = jnp.where(m_ref[8 - tap : 9 - tap, :] > 0, moved, 0.0)
        d_ref[rows * tap : rows * (tap + 1), :] = moved.astype(d_ref.dtype)
    for start in range(0, cells, CHUNK):
        dx_ref[:, start : start + CHUNK] = jnp.dot(
            wt_ref[...], d_ref[:, start : start + CHUNK], preferred_element_type=jnp.float32
        ).astype(dx_ref.dtype)
    for start in range(0, x_in.shape[0], 256):
        g_ref[:, start : start + 256] = lax.dot_general(
            d_ref[...],
            x_in[start : start + 256, :],
            (((1,), (1,)), ((), ())),
            preferred_element_type=jnp.float32,
        ).astype(g_ref.dtype)


def first_back_body(number, dy_ref, n_ref, rstd_ref, gb_ref, p_ref, g_ref, s_ref):
    dv, d_gain, d_bias = norm_slope(
        number, dy_ref[...], n_ref[...], rstd_ref[:, 0:1], gb_ref[:, 0:1], gb_ref[:, 1:2]
    )
    lanes = lax.broadcasted_iota(jnp.int32, s_ref.shape, 1)
    s_ref[...] = jnp.where(lanes == 0, d_gain, d_bias)
    blocks, size = p_ref.shape[0], p_ref.shape[1]
    total = jnp.zeros(g_ref.shape, jnp.float32)
    for block in range(blocks):
        shift = (-block * size) % dv.shape[1]
        piece = (pltpu.roll(dv, shift, 1) if shift else dv)[:, :size]
        total = total + jnp.dot(
            piece.astype(p_ref.dtype), p_ref[block], preferred_element_type=jnp.float32
        )
    g_ref[...] = total.astype(g_ref.dtype)


BIG = pltpu.CompilerParams(vmem_limit_bytes=48 << 20)


def first_block(pixels, w, gb, masks, number):
    rows, cells = w.shape[0], masks.shape[1]
    return pl.pallas_call(
        functools.partial(first_body, number),
        name="stem_first",
        out_shape=(
            jax.ShapeDtypeStruct((rows, cells), jnp.float32),
            jax.ShapeDtypeStruct((rows, 128), jnp.float32),
            jax.ShapeDtypeStruct((rows, cells), jnp.float32),
            jax.ShapeDtypeStruct((PORTIONS, GROUP, cells), LOW),
        ),
        scratch_shapes=[pltpu.VMEM((rows, cells), jnp.float32)],
        compiler_params=BIG,
    )(pixels, w, gb, masks)


def conv_block(layer, x_all, w, gb, masks, y, number):
    rows, cells = y.shape
    return pl.pallas_call(
        functools.partial(conv_body, number, layer),
        name="stem_conv",
        out_shape=(
            jax.ShapeDtypeStruct((rows, cells), jnp.float32),
            jax.ShapeDtypeStruct((rows, 128), jnp.float32),
            jax.ShapeDtypeStruct((rows, cells), jnp.float32),
            jax.ShapeDtypeStruct((PORTIONS, GROUP, cells), LOW),
        ),
        scratch_shapes=[pltpu.VMEM((9 * rows, cells), jnp.float32)],
        compiler_params=BIG,
    )(x_all, w, gb, masks, y)


def conv_block_back(layer, dy, normed, rstd, gb, masks, x_all, w_t, number):
    rows, cells = dy.shape
    features = x_all.shape[0]
    return pl.pallas_call(
        functools.partial(conv_back_body, number, layer),
        name="stem_conv_back",
        out_shape=(
            jax.ShapeDtypeStruct((features, cells), LOW),
            jax.ShapeDtypeStruct((9 * rows, features), LOW),
            jax.ShapeDtypeStruct((rows, 128), jnp.float32),
        ),
        scratch_shapes=[pltpu.VMEM((9 * rows, cells), LOW)],
        compiler_params=BIG,
    )(dy, normed, rstd, gb, masks, x_all, w_t)


def first_block_back(dy, normed, rstd, gb, pixels, number):
    rows, cells = dy.shape
    return pl.pallas_call(
        functools.partial(first_back_body, number),
        name="stem_first_back",
        out_shape=(
            jax.ShapeDtypeStruct((rows, pixels.shape[2]), LOW),
            jax.ShapeDtypeStruct((rows, 128), jnp.float32),
        ),
        compiler_params=BIG,
    )(dy, normed, rstd, gb, pixels)


def padded_2(cells, sides, width):
    for axis, dim in sides:
        count = lax.axis_size(axis)
        ends = count - 1
        head = lax.slice_in_dim(cells, 0, width, axis=dim)
        tail = lax.slice_in_dim(cells, cells.shape[dim] - width, cells.shape[dim], axis=dim)
        cells = jnp.concatenate(
            [
                lax.ppermute(tail, axis, [(i, (i + 1) % count) for i in range(ends)]),
                cells,
                lax.ppermute(head, axis, [((i + 1) % count, i) for i in range(ends)]),
            ],
            axis=dim,
        )
    return cells


def passed_along(array, axis, by):
    length = lax.axis_size(axis)
    pairs = [(i, i + by) for i in range(length) if 0 <= i + by < length]
    return lax.ppermute(array, axis, pairs)


def layer_norm(activ, gain_vec, bias_vec):
    row_mean = jnp.mean(activ, -1, keepdims=True)
    centred = activ - row_mean
    spread = jnp.mean(centred * centred, -1, keepdims=True)
    return centred * lax.rsqrt(spread + 1e-06) * gain_vec + bias_vec


def heads_of(matrix):
    return matrix.reshape(matrix.shape[0], HEADS, -1)


def dot_float(left, right):
    return jnp.dot(left, right, preferred_element_type=jnp.float32)


def norm_batch(values, gain_vec, bias_vec, number):
    sums = lax.psum((jnp.sum(values, 0), jnp.sum(values * values, 0)), ("dp", "seq"))
    col_mean = sums[0] / number
    col_var = sums[1] / number - col_mean * col_mean
    inv_std = lax.rsqrt(col_var + 1e-05)
    normed = (values - col_mean) * inv_std
    return (normed, inv_std, normed * gain_vec + bias_vec)


def batch_back(d_pre, normed, inv_std, gain_vec, number):
    grad_gain = jnp.sum(d_pre * normed, 0)
    grad_bias = jnp.sum(d_pre, 0)
    d_normed = d_pre * gain_vec
    sums = lax.psum((jnp.sum(d_normed, 0), jnp.sum(d_normed * normed, 0)), ("dp", "seq"))
    d_values = inv_std * (d_normed - sums[0] / number - normed * (sums[1] / number))
    return (d_values, grad_gain, grad_bias)


def conv_fwd(flat_low, weight):
    features = flat_low.shape[1]
    grid_rows = flat_low.shape[0] // SIDE
    grid = flat_low.reshape(grid_rows, SIDE, features)
    padded = padded_2(grid, (("seq", 0),), 1)
    padded = jnp.pad(padded, ((0, 0), (1, 1), (0, 0)))
    total = jnp.zeros((grid_rows * SIDE, features), jnp.float32)
    for row_tap in range(3):
        for col_tap in range(3):
            tap = 3 * row_tap + col_tap
            window = padded[row_tap : row_tap + grid_rows, col_tap : col_tap + SIDE].reshape(
                -1, features
            )
            total = total + dot_float(window, weight[tap * features : (tap + 1) * features])
    return (total, padded)


def send_rim(rim_rows, offset):
    return passed_along(rim_rows.astype(jnp.bfloat16), "seq", offset).astype(rim_rows.dtype)


def conv_back(padded, d_out_low, weight):
    features = d_out_low.shape[1]
    grid_rows = padded.shape[0] - 2
    d_padded = jnp.zeros((grid_rows + 2, SIDE + 2, features), jnp.float32)
    tap_grads = []
    for row_tap in range(3):
        for col_tap in range(3):
            tap = 3 * row_tap + col_tap
            tap_weight = weight[tap * features : (tap + 1) * features]
            window = padded[row_tap : row_tap + grid_rows, col_tap : col_tap + SIDE].reshape(
                -1, features
            )
            tap_grads.append(dot_float(window.T, d_out_low))
            spread = dot_float(d_out_low, tap_weight.T).reshape(grid_rows, SIDE, features)
            d_padded = d_padded + jnp.pad(
                spread, ((row_tap, 2 - row_tap), (col_tap, 2 - col_tap), (0, 0))
            )
    inner = d_padded[1 : grid_rows + 1, 1 : SIDE + 1]
    from_below = send_rim(d_padded[0, 1 : SIDE + 1], -1)
    from_above = send_rim(d_padded[grid_rows + 1, 1 : SIDE + 1], 1)
    inner = inner.at[grid_rows - 1].add(from_below).at[0].add(from_above)
    return (jnp.concatenate(tap_grads, 0), inner.reshape(-1, features))


def attend_block(queries, key_rows, value_rows, allowed, score_scale):
    scores = (
        jnp.einsum("qhd,khd->hqk", queries, key_rows, preferred_element_type=jnp.float32)
        * score_scale
    )
    scores = jnp.where(allowed[None], scores, -1000000000.0)
    row_max = jnp.max(scores, -1, keepdims=True)
    exponent = jnp.exp(scores - row_max)
    row_total = jnp.sum(exponent, -1, keepdims=True)
    softmax = (exponent / row_total).astype(jnp.bfloat16)
    outputs = jnp.einsum("hqk,khd->qhd", softmax, value_rows, preferred_element_type=jnp.float32)
    return (outputs, row_max + jnp.log(row_total))


def attend_back(queries, key_rows, value_rows, allowed, score_scale, grad_out, log_total):
    scores = (
        jnp.einsum("qhd,khd->hqk", queries, key_rows, preferred_element_type=jnp.float32)
        * score_scale
    )
    scores = jnp.where(allowed[None], scores, -1000000000.0)
    softmax = jnp.exp(scores - log_total)
    d_softmax = jnp.einsum("qhd,khd->hqk", grad_out, value_rows, preferred_element_type=jnp.float32)
    row_delta = jnp.sum(softmax * d_softmax, -1, keepdims=True)
    d_scores = (softmax * (d_softmax - row_delta)).astype(jnp.bfloat16)
    d_query = (
        jnp.einsum("hqk,khd->qhd", d_scores, key_rows, preferred_element_type=jnp.float32)
        * score_scale
    )
    d_keys = (
        jnp.einsum("hqk,qhd->khd", d_scores, queries, preferred_element_type=jnp.float32)
        * score_scale
    )
    d_values = jnp.einsum(
        "hqk,qhd->khd", softmax.astype(jnp.bfloat16), grad_out, preferred_element_type=jnp.float32
    )
    return (d_query, d_keys, d_values)


def run_attention(queries, key_rows, value_rows, allow_fn, score_scale):
    row_count = queries.shape[0]
    block_rows = min(512, row_count)
    block_count = row_count // block_rows
    query_blocks = queries.reshape(block_count, block_rows, queries.shape[1], queries.shape[2])
    starts = jnp.arange(block_count, dtype=jnp.int32) * block_rows

    def one_block(block_pair):
        return attend_block(
            block_pair[0], key_rows, value_rows, allow_fn(block_pair[1], block_rows), score_scale
        )

    outputs, log_total = lax.map(one_block, (query_blocks, starts))
    return (outputs.reshape(queries.shape), log_total)


def run_back(queries, key_rows, value_rows, allow_fn, score_scale, grad_out, log_total):
    row_count = queries.shape[0]
    block_rows = min(512, row_count)
    block_count = row_count // block_rows
    query_blocks = queries.reshape(block_count, block_rows, queries.shape[1], queries.shape[2])
    grad_blocks = grad_out.reshape(query_blocks.shape)
    starts = jnp.arange(block_count, dtype=jnp.int32) * block_rows

    def one_block(running, block_items):
        query_part, grad_part, total_part, first_row = block_items
        d_query, d_keys, d_values = attend_back(
            query_part,
            key_rows,
            value_rows,
            allow_fn(first_row, block_rows),
            score_scale,
            grad_part,
            total_part,
        )
        return ((running[0] + d_keys, running[1] + d_values), d_query)

    zero_grads = jnp.zeros(key_rows.shape, jnp.float32)
    sums_kv, d_query = lax.scan(
        one_block, (zero_grads, zero_grads), (query_blocks, grad_blocks, log_total, starts)
    )
    return (d_query.reshape(queries.shape), sums_kv[0], sums_kv[1])


def general_device(
    captions,
    patches,
    prefix,
    prefix_count,
    caption_len,
    cotangent,
    w_patch,
    w_conv,
    w_self_qkv,
    w_self_out,
    w_cross_q,
    w_cross_kv,
    w_cross_out,
    w_up,
    w_down,
    norm_params,
):
    gathered = (
        lax.all_gather(w_patch, "dp", axis=0, tiled=True),
        lax.all_gather(w_conv, "dp", axis=1, tiled=True),
        lax.all_gather(w_self_qkv, "dp", axis=0, tiled=True),
        lax.all_gather(w_self_out, "dp", axis=0, tiled=True),
        lax.all_gather(w_cross_q, "dp", axis=0, tiled=True),
        lax.all_gather(w_cross_kv, "dp", axis=0, tiled=True),
        lax.all_gather(w_cross_out, "dp", axis=0, tiled=True),
        lax.all_gather(w_up, "dp", axis=0, tiled=True),
        lax.all_gather(w_down, "dp", axis=0, tiled=True),
        lax.all_gather(norm_params, "dp", axis=1, tiled=True),
    )
    (
        full_patch,
        full_conv,
        full_qkv,
        full_sout,
        full_cq,
        full_ckv,
        full_cout,
        full_up,
        full_down,
        full_norms,
    ) = gathered
    norms = full_norms.astype(jnp.float32)
    features = full_sout.shape[0]
    score_scale = (features // HEADS) ** (-0.5)
    seq_count = lax.axis_size("seq")
    seq_index = lax.axis_index("seq")
    pixels = patches[0]
    stem_out = dot_float(pixels, full_patch)
    number = stem_out.shape[0] * lax.axis_size("dp") * seq_count
    normed_one, inv_one, pre_one = norm_batch(stem_out, norms[0], norms[1], number)
    first_out = jax.nn.gelu(pre_one)
    first_low = first_out.astype(jnp.bfloat16)
    conv_two, padded_two = conv_fwd(first_low, full_conv[0])
    normed_two, inv_two, pre_two = norm_batch(conv_two, norms[2], norms[3], number)
    second_out = first_out + jax.nn.gelu(pre_two)
    second_low = second_out.astype(jnp.bfloat16)
    conv_three, padded_three = conv_fwd(second_low, full_conv[1])
    normed_three, inv_three, pre_three = norm_batch(conv_three, norms[4], norms[5], number)
    third_out = second_out + jax.nn.gelu(pre_three)
    patch_low = third_out.astype(jnp.bfloat16)
    prefix_low = prefix[0]
    kv_prefix = dot_float(prefix_low, full_ckv).astype(jnp.bfloat16)
    kv_patch = dot_float(patch_low, full_ckv).astype(jnp.bfloat16)
    all_prefix, all_patch = (
        lax.all_gather(kv_prefix, "seq", axis=0, tiled=True),
        lax.all_gather(kv_patch, "seq", axis=0, tiled=True),
    )
    memory_kv = jnp.concatenate([all_prefix, all_patch], 0)
    mem_rows = memory_kv.shape[0]
    prefix_total = all_prefix.shape[0]
    mem_keys = heads_of(memory_kv[:, :features])
    mem_values = heads_of(memory_kv[:, features:])
    slot_ids = jnp.arange(mem_rows, dtype=jnp.int32)
    mem_allowed = (slot_ids >= prefix_total) | (slot_ids < prefix_count[0])

    def cross_allow(first_row, block_rows):
        return jnp.broadcast_to(mem_allowed[None], (block_rows, mem_rows))

    inputs = captions[0].astype(jnp.float32)
    row_count = inputs.shape[0]
    low_one = layer_norm(inputs, norms[6], norms[7]).astype(jnp.bfloat16)
    qkv = dot_float(low_one, full_qkv).astype(jnp.bfloat16)
    queries = heads_of(qkv[:, :features])
    own_keys = heads_of(qkv[:, features : 2 * features])
    own_values = heads_of(qkv[:, 2 * features :])
    key_parts = [own_keys]
    value_parts = [own_values]
    position_parts = [seq_index * row_count + jnp.arange(row_count, dtype=jnp.int32)]
    offset = 1
    got_keys, got_values = passed_along((own_keys, own_values), "seq", offset)
    key_parts.insert(0, got_keys)
    value_parts.insert(0, got_values)
    position_parts.insert(
        0, (seq_index - offset) * row_count + jnp.arange(row_count, dtype=jnp.int32)
    )
    all_keys = jnp.concatenate(key_parts, 0)
    all_values = jnp.concatenate(value_parts, 0)
    key_pos = jnp.concatenate(position_parts, 0)
    length_one = caption_len[0]

    def self_allow(first_row, block_rows):
        query_pos = seq_index * row_count + first_row + jnp.arange(block_rows, dtype=jnp.int32)
        return (
            (key_pos[None] <= query_pos[:, None])
            & (key_pos[None] >= 0)
            & (key_pos[None] < length_one)
        )

    self_out, self_total = run_attention(queries, all_keys, all_values, self_allow, score_scale)
    self_low = self_out.reshape(row_count, features).astype(jnp.bfloat16)
    after_self = inputs + dot_float(self_low, full_sout)
    low_two = layer_norm(after_self, norms[8], norms[9]).astype(jnp.bfloat16)
    cross_flat = dot_float(low_two, full_cq).astype(jnp.bfloat16)
    cross_q = heads_of(cross_flat)
    cross_out, cross_total = run_attention(cross_q, mem_keys, mem_values, cross_allow, score_scale)
    cross_low = cross_out.reshape(row_count, features).astype(jnp.bfloat16)
    after_cross = after_self + dot_float(cross_low, full_cout)
    low_three = layer_norm(after_cross, norms[10], norms[11]).astype(jnp.bfloat16)
    up_proj = dot_float(low_three, full_up)
    hidden_low = jax.nn.gelu(up_proj).astype(jnp.bfloat16)
    result = after_cross + dot_float(hidden_low, full_down)
    back_weights = (
        lax.all_gather(w_patch, "dp", axis=0, tiled=True),
        lax.all_gather(w_conv, "dp", axis=1, tiled=True),
        lax.all_gather(w_self_qkv, "dp", axis=0, tiled=True),
        lax.all_gather(w_self_out, "dp", axis=0, tiled=True),
        lax.all_gather(w_cross_q, "dp", axis=0, tiled=True),
        lax.all_gather(w_cross_kv, "dp", axis=0, tiled=True),
        lax.all_gather(w_cross_out, "dp", axis=0, tiled=True),
        lax.all_gather(w_up, "dp", axis=0, tiled=True),
        lax.all_gather(w_down, "dp", axis=0, tiled=True),
        lax.all_gather(norm_params, "dp", axis=1, tiled=True),
    )
    (
        back_patch,
        back_conv,
        back_qkv,
        back_sout,
        back_cq,
        back_ckv,
        back_cout,
        back_up,
        back_down,
        back_norms,
    ) = back_weights
    bnorms = back_norms.astype(jnp.float32)
    out_grad = cotangent[0].astype(jnp.float32)
    grad_low = cotangent[0]
    grad_down = dot_float(hidden_low.T, grad_low)
    d_hidden = dot_float(grad_low, back_down.T)
    unused_gelu, gelu_back = jax.vjp(jax.nn.gelu, up_proj)
    d_upper = gelu_back(d_hidden)[0].astype(jnp.bfloat16)
    grad_up = dot_float(low_three.T, d_upper)
    unused_three, norm_back_three = jax.vjp(layer_norm, after_cross, bnorms[10], bnorms[11])
    d_three, grad_gain_three, grad_bias_three = norm_back_three(dot_float(d_upper, back_up.T))
    d_after_cross = out_grad + d_three
    cross_grad_low = d_after_cross.astype(jnp.bfloat16)
    grad_cout = dot_float(cross_low.T, cross_grad_low)
    d_cross = heads_of(dot_float(cross_grad_low, back_cout.T).astype(jnp.bfloat16))
    d_cross_q, d_mem_keys, d_mem_values = run_back(
        cross_q, mem_keys, mem_values, cross_allow, score_scale, d_cross, cross_total
    )
    d_cross_low = d_cross_q.reshape(row_count, features).astype(jnp.bfloat16)
    grad_cq = dot_float(low_two.T, d_cross_low)
    unused_two, norm_back_two = jax.vjp(layer_norm, after_self, bnorms[8], bnorms[9])
    d_two, grad_gain_two, grad_bias_two = norm_back_two(dot_float(d_cross_low, back_cq.T))
    d_after_self = d_after_cross + d_two
    d_memory = jnp.concatenate(
        [d_mem_keys.reshape(mem_rows, features), d_mem_values.reshape(mem_rows, features)], 1
    )
    mine_prefix, mine_patch = (
        lax.psum_scatter(
            d_memory[:prefix_total].astype(jnp.bfloat16), "seq", scatter_dimension=0, tiled=True
        ).astype(jnp.float32),
        lax.psum_scatter(
            d_memory[prefix_total:].astype(jnp.bfloat16), "seq", scatter_dimension=0, tiled=True
        ).astype(jnp.float32),
    )
    mine_prefix_low = mine_prefix.astype(jnp.bfloat16)
    mine_patch_low = mine_patch.astype(jnp.bfloat16)
    grad_ckv = dot_float(prefix_low.T, mine_prefix_low) + dot_float(patch_low.T, mine_patch_low)
    prefix_back = dot_float(mine_prefix_low, back_ckv.T)
    d_third = dot_float(mine_patch_low, back_ckv.T)
    unused_act_three, act_back_three = jax.vjp(jax.nn.gelu, pre_three)
    d_conv_three, grad_gain_bn3, grad_bias_bn3 = batch_back(
        act_back_three(d_third)[0], normed_three, inv_three, bnorms[4], number
    )
    grad_conv_one, d_second_in = conv_back(
        padded_three, d_conv_three.astype(jnp.bfloat16), back_conv[1]
    )
    d_second = d_third + d_second_in
    unused_act_two, act_back_two = jax.vjp(jax.nn.gelu, pre_two)
    d_conv_two, grad_gain_bn2, grad_bias_bn2 = batch_back(
        act_back_two(d_second)[0], normed_two, inv_two, bnorms[2], number
    )
    grad_conv_zero, d_first_in = conv_back(
        padded_two, d_conv_two.astype(jnp.bfloat16), back_conv[0]
    )
    d_first = d_second + d_first_in
    unused_act_one, act_back_one = jax.vjp(jax.nn.gelu, pre_one)
    d_stem, grad_gain_bn1, grad_bias_bn1 = batch_back(
        act_back_one(d_first)[0], normed_one, inv_one, bnorms[0], number
    )
    grad_patch = dot_float(pixels.T, d_stem.astype(jnp.bfloat16))
    grad_conv = jnp.stack([grad_conv_zero, grad_conv_one])
    self_grad_low = d_after_self.astype(jnp.bfloat16)
    grad_sout = dot_float(self_low.T, self_grad_low)
    d_self = heads_of(dot_float(self_grad_low, back_sout.T).astype(jnp.bfloat16))
    d_query, d_all_keys, d_all_values = run_back(
        queries, all_keys, all_values, self_allow, score_scale, d_self, self_total
    )
    own_start = (seq_count - 1) * row_count
    own_dkeys = d_all_keys[own_start:]
    own_dvalues = d_all_values[own_start:]
    offset = 1
    piece_start = (seq_count - 1 - offset) * row_count
    back_keys = passed_along(
        d_all_keys[piece_start : piece_start + row_count].astype(jnp.bfloat16), "seq", -offset
    ).astype(jnp.float32)
    back_values = passed_along(
        d_all_values[piece_start : piece_start + row_count].astype(jnp.bfloat16), "seq", -offset
    ).astype(jnp.float32)
    own_dkeys = own_dkeys + back_keys
    own_dvalues = own_dvalues + back_values
    d_qkv = jnp.concatenate(
        [
            d_query.reshape(row_count, features),
            own_dkeys.reshape(row_count, features),
            own_dvalues.reshape(row_count, features),
        ],
        1,
    ).astype(jnp.bfloat16)
    grad_qkv = dot_float(low_one.T, d_qkv)
    unused_one, norm_back_one = jax.vjp(layer_norm, inputs, bnorms[6], bnorms[7])
    d_one, grad_gain_one, grad_bias_one = norm_back_one(dot_float(d_qkv, back_qkv.T))
    d_inputs = d_after_self + d_one
    grad_norms = jnp.stack(
        [
            grad_gain_bn1,
            grad_bias_bn1,
            grad_gain_bn2,
            grad_bias_bn2,
            grad_gain_bn3,
            grad_bias_bn3,
            grad_gain_one,
            grad_bias_one,
            grad_gain_two,
            grad_bias_two,
            grad_gain_three,
            grad_bias_three,
        ]
    )
    shard_sums = (
        lax.psum_scatter(grad_patch, "dp", scatter_dimension=0, tiled=True),
        lax.psum_scatter(grad_conv, "dp", scatter_dimension=1, tiled=True),
        lax.psum_scatter(grad_qkv, "dp", scatter_dimension=0, tiled=True),
        lax.psum_scatter(grad_sout, "dp", scatter_dimension=0, tiled=True),
        lax.psum_scatter(grad_cq, "dp", scatter_dimension=0, tiled=True),
        lax.psum_scatter(grad_ckv, "dp", scatter_dimension=0, tiled=True),
        lax.psum_scatter(grad_cout, "dp", scatter_dimension=0, tiled=True),
        lax.psum_scatter(grad_up, "dp", scatter_dimension=0, tiled=True),
        lax.psum_scatter(grad_down, "dp", scatter_dimension=0, tiled=True),
        lax.psum_scatter(grad_norms, "dp", scatter_dimension=1, tiled=True),
    )
    totals = (
        lax.psum(shard_sums[0].astype(jnp.bfloat16), "seq").astype(jnp.float32),
        lax.psum(shard_sums[1].astype(jnp.bfloat16), "seq").astype(jnp.float32),
        lax.psum(shard_sums[2].astype(jnp.bfloat16), "seq").astype(jnp.float32),
        lax.psum(shard_sums[3].astype(jnp.bfloat16), "seq").astype(jnp.float32),
        lax.psum(shard_sums[4].astype(jnp.bfloat16), "seq").astype(jnp.float32),
        lax.psum(shard_sums[5].astype(jnp.bfloat16), "seq").astype(jnp.float32),
        lax.psum(shard_sums[6].astype(jnp.bfloat16), "seq").astype(jnp.float32),
        lax.psum(shard_sums[7].astype(jnp.bfloat16), "seq").astype(jnp.float32),
        lax.psum(shard_sums[8].astype(jnp.bfloat16), "seq").astype(jnp.float32),
        lax.psum(shard_sums[9].astype(jnp.bfloat16), "seq").astype(jnp.float32),
    )
    return (
        result[None].astype(jnp.bfloat16),
        d_inputs[None].astype(jnp.bfloat16),
        prefix_back[None].astype(jnp.bfloat16),
        totals[0],
        totals[1],
        totals[2],
        totals[3],
        totals[4],
        totals[5],
        totals[6],
        totals[7],
        totals[8],
        totals[9],
    )


PAIR = 128


def head_lanes(array, which, width):
    lanes = lax.broadcasted_iota(jnp.int32, array.shape, 1)
    return jnp.where((lanes >= which * width) & (lanes < (which + 1) * width), array, 0)


def scores_t(keys, q_head):
    return lax.dot_general(
        keys, q_head, (((1,), (1,)), ((), ())), preferred_element_type=jnp.float32
    )


def masked_scores(kind, info_ref, ok_ref, keys, q_head):
    if kind == "cross":
        scores = scores_t(keys, q_head)
        return jnp.where(ok_ref[:, 0:1] > 0, scores, -1e9)
    half = keys.shape[0] // 2
    before = scores_t(keys[:half], q_head)
    own = scores_t(keys[half:], q_head)
    before = jnp.where(info_ref[0] > 0, before, -1e9)
    key_at = lax.broadcasted_iota(jnp.int32, own.shape, 0)
    query_at = lax.broadcasted_iota(jnp.int32, own.shape, 1)
    own = jnp.where((key_at <= query_at) & (key_at < info_ref[1]), own, -1e9)
    return jnp.concatenate([before, own], 0)


def attend_body(kind, width, info_ref, ok_ref, q_ref, k_ref, v_ref, o_ref, lse_ref):
    keys, values = k_ref[...], v_ref[...]
    outs = []
    for which in range(PAIR // width):
        q_head = head_lanes(q_ref[...], which, width)
        scores = masked_scores(kind, info_ref, ok_ref, keys, q_head)
        top = jnp.max(scores, 0, keepdims=True)
        weights = jnp.exp(scores - top)
        total = jnp.sum(weights, 0, keepdims=True)
        lse_ref[0, which : which + 1, :] = top + jnp.log(total)
        out_t = lax.dot_general(
            head_lanes(values, which, width),
            weights.astype(LOW),
            (((0,), (0,)), ((), ())),
            preferred_element_type=jnp.float32,
        )
        outs.append(out_t / total)
    o_ref[...] = (outs[0] + outs[1]).T.astype(o_ref.dtype)


def attend_back_body(
    kind, width, scale, info_ref, ok_ref, q_ref, k_ref, v_ref, do_ref, lse_ref, dq_ref, dk_ref, dv_ref
):
    keys, values = k_ref[...], v_ref[...]
    dq_t, dk, dv = None, None, None
    for which in range(PAIR // width):
        q_head = head_lanes(q_ref[...], which, width)
        do_head = head_lanes(do_ref[...], which, width)
        scores = masked_scores(kind, info_ref, ok_ref, keys, q_head)
        probs = jnp.exp(scores - lse_ref[0, which : which + 1, :])
        d_probs = scores_t(values, do_head)
        delta = jnp.sum(probs * d_probs, 0, keepdims=True)
        ds = (probs * (d_probs - delta)).astype(LOW)
        part_k = jnp.dot(ds, q_head, preferred_element_type=jnp.float32)
        part_v = jnp.dot(probs.astype(LOW), do_head, preferred_element_type=jnp.float32)
        part_q = lax.dot_general(
            head_lanes(keys, which, width),
            ds,
            (((0,), (0,)), ((), ())),
            preferred_element_type=jnp.float32,
        )
        dk = part_k if dk is None else dk + part_k
        dv = part_v if dv is None else dv + part_v
        dq_t = part_q if dq_t is None else dq_t + part_q
    dq_ref[...] = (dq_t * scale).T.astype(dq_ref.dtype)
    dk_ref[...] = dk.astype(dk_ref.dtype)
    dv_ref[...] = dv.astype(dv_ref.dtype)


def attention_specs(rows, keys, ok):
    return [
        pl.BlockSpec(memory_space=pltpu.SMEM),
        pl.BlockSpec(ok.shape, lambda i: (0, 0)),
        pl.BlockSpec((rows, PAIR), lambda i: (0, i)),
        pl.BlockSpec((keys, PAIR), lambda i: (0, i)),
        pl.BlockSpec((keys, PAIR), lambda i: (0, i)),
    ]


def attend(kind, info, ok, q, k, v):
    rows, features = q.shape
    keys = k.shape[0]
    width = features // HEADS
    pairs = features // PAIR
    return pl.pallas_call(
        functools.partial(attend_body, kind, width),
        name=kind + "_attend",
        grid=(pairs,),
        in_specs=attention_specs(rows, keys, ok),
        out_specs=(
            pl.BlockSpec((rows, PAIR), lambda i: (0, i)),
            pl.BlockSpec((1, 8, rows), lambda i: (i, 0, 0)),
        ),
        out_shape=(
            jax.ShapeDtypeStruct((rows, features), LOW),
            jax.ShapeDtypeStruct((pairs, 8, rows), jnp.float32),
        ),
        compiler_params=BIG,
        cost_estimate=pl.CostEstimate(
            flops=4 * rows * keys * features, bytes_accessed=2 * (2 * rows + 2 * keys) * features,
            transcendentals=rows * keys * HEADS,
        ),
    )(info, ok, q, k, v)


def attend_grads(kind, info, ok, q, k, v, d_out, lse, scale):
    rows, features = q.shape
    keys = k.shape[0]
    width = features // HEADS
    pairs = features // PAIR
    return pl.pallas_call(
        functools.partial(attend_back_body, kind, width, scale),
        name=kind + "_attend_back",
        grid=(pairs,),
        in_specs=attention_specs(rows, keys, ok)
        + [
            pl.BlockSpec((rows, PAIR), lambda i: (0, i)),
            pl.BlockSpec((1, 8, rows), lambda i: (i, 0, 0)),
        ],
        out_specs=(
            pl.BlockSpec((rows, PAIR), lambda i: (0, i)),
            pl.BlockSpec((keys, PAIR), lambda i: (0, i)),
            pl.BlockSpec((keys, PAIR), lambda i: (0, i)),
        ),
        out_shape=(
            jax.ShapeDtypeStruct((rows, features), LOW),
            jax.ShapeDtypeStruct((keys, features), LOW),
            jax.ShapeDtypeStruct((keys, features), LOW),
        ),
        compiler_params=BIG,
        cost_estimate=pl.CostEstimate(
            flops=10 * rows * keys * features, bytes_accessed=2 * (3 * rows + 6 * keys) * features,
            transcendentals=rows * keys * HEADS,
        ),
    )(info, ok, q, k, v, d_out, lse)


def weight_grads_body(jobs, targets, owners, *refs):
    count = len(refs) - 4
    ins, (o_ref, left_ref, right_ref, sum_ref) = refs[:count], refs[count:]
    step = pl.program_id(0)
    for at, (left, right, rows, row_at, left_col, right_col) in enumerate(jobs):

        @pl.when(step == at)
        def _():
            size = left_ref.shape[1]
            left_ref[:rows] = ins[left][row_at : row_at + rows, left_col : left_col + size]
            right_ref[:rows] = ins[right][row_at : row_at + rows, right_col : right_col + size]
            if rows < left_ref.shape[0]:
                left_ref[rows:] = jnp.zeros((left_ref.shape[0] - rows, size), left_ref.dtype)
                right_ref[rows:] = jnp.zeros((left_ref.shape[0] - rows, size), left_ref.dtype)

    product = lax.dot_general(
        left_ref[...], right_ref[...], (((0,), (0,)), ((), ())), preferred_element_type=jnp.float32
    )
    for at, target in enumerate(targets):
        if at and targets[at - 1] == target:

            @pl.when(step == at)
            def _():
                sum_ref[...] += product

        else:

            @pl.when(step == at)
            def _():
                sum_ref[...] = product

    put_grads(owners, targets, step, o_ref, sum_ref)


def put_grads(owners, targets, step, o_ref, sum_ref):
    total = sum_ref[...].astype(o_ref.dtype)
    if owners == "mlp":
        tall = total.shape[0] // 4

        @pl.when(step < 4)
        def _():
            for part in range(4):
                o_ref[2 * (4 * step + part)] = total[tall * part : tall * (part + 1)]

        @pl.when(step >= 4)
        def _():
            short = total.shape[0] // 16
            start = pl.multiple_of(short * (step - 4), short)
            for a in range(16):
                o_ref[2 * a + 1, pl.ds(start, short)] = total[short * a : short * (a + 1)]

    else:
        first_twice = len(targets) - 4
        target = jnp.where(step < first_twice, step, first_twice + (step - first_twice) // 2)
        short = total.shape[0] // 16
        start = pl.multiple_of(short * lax.rem(target, 4), short)
        for a in range(16):
            o_ref[2 * a + target // 4, pl.ds(start, short)] = total[short * a : short * (a + 1)]


def weight_grads(jobs, targets, owners, arrays, features, rows):
    return pl.pallas_call(
        functools.partial(weight_grads_body, tuple(jobs), tuple(targets), owners),
        name="weight_grads",
        grid=(len(jobs),),
        in_specs=[pl.BlockSpec(memory_space=pltpu.VMEM)] * len(arrays),
        out_specs=pl.BlockSpec(memory_space=pltpu.VMEM),
        out_shape=jax.ShapeDtypeStruct((32, features // 4, features), LOW),
        scratch_shapes=[
            pltpu.VMEM((rows, features), LOW),
            pltpu.VMEM((rows, features), LOW),
            pltpu.VMEM((features, features), jnp.float32),
        ],
        compiler_params=BIG,
        cost_estimate=pl.CostEstimate(
            flops=2 * len(jobs) * rows * features * features,
            bytes_accessed=2 * 8 * features * features,
            transcendentals=0,
        ),
    )(*arrays)


def low_dot(left, right):
    return dot_float(left, right).astype(LOW)


def dot_t(left, right):
    return lax.dot_general(left, right, (((1,), (1,)), ((), ())), preferred_element_type=jnp.float32)


def t_dot(left, right):
    return lax.dot_general(left, right, (((0,), (0,)), ((), ())), preferred_element_type=jnp.float32)


def stem_weight_blocks(w_conv, w_patch, norm_params, s):
    features = w_patch.shape[1]
    flat = jnp.concatenate([w_conv.reshape(-1, features), w_patch], 0).T
    blocks = slots_to_devices(flat.reshape(PORTIONS, 32, GROUP, flat.shape[1]))
    blocks = blocks.reshape(16, 2, PORTIONS * GROUP, flat.shape[1])
    blocks = lax.dynamic_index_in_dim(blocks, s, 1, keepdims=False)
    rows = PORTIONS * GROUP
    extra = jnp.pad(norm_params, ((0, rows - norm_params.shape[0]), (0, 0)))
    blocks = jnp.concatenate([blocks, jnp.broadcast_to(extra, (16,) + extra.shape)], 2)
    return blocks


def stem_weights(got, w_conv, w_patch, norm_params):
    depth, conv_rows, features = w_conv.shape
    rows = PORTIONS * GROUP
    convs = []
    for layer in range(depth):
        part = got[:, :, layer * conv_rows : (layer + 1) * conv_rows]
        part = part.transpose(1, 0, 2).reshape(rows, 9, features).transpose(1, 0, 2)
        convs.append(part.reshape(9 * rows, features))
    at = depth * conv_rows
    patch = got[:, :, at : at + w_patch.shape[0]].transpose(1, 0, 2).reshape(rows, -1)
    norms = got[:, : norm_params.shape[0], at + w_patch.shape[0] :]
    return convs, patch, norms.transpose(1, 0, 2).reshape(norm_params.shape[0], -1)


def own_columns(norms):
    bits = my_bits()
    cut = norms.reshape(norms.shape[0], PORTIONS, 32, GROUP)
    parts = [
        lax.dynamic_index_in_dim(cut[:, p], slot_of(bits, p), 1, keepdims=False)
        for p in range(PORTIONS)
    ]
    mine = jnp.concatenate(parts, 1).T
    return jnp.pad(mine, ((0, 0), (0, 128 - mine.shape[1])))


def fast_device(
    captions,
    patches,
    prefix,
    prefix_count,
    caption_len,
    cotangent,
    w_patch,
    w_conv,
    w_self_qkv,
    w_self_out,
    w_cross_q,
    w_cross_kv,
    w_cross_out,
    w_up,
    w_down,
    norm_params,
):
    a_index, s_index = lax.axis_index("dp"), lax.axis_index("seq")
    examples, halves = 16, 2
    features = w_self_out.shape[1]
    score_scale = (features // HEADS) ** (-0.5)

    def chunks(w):
        return [w[:, i * features : (i + 1) * features] for i in range(w.shape[1] // features)]

    shard_rows = w_patch.shape[0]
    pieces = [(0, 0, features * i) for i in range(3)] + [(1, 0, 0), (2, 0, 0)]
    pieces += [(3, 0, 0), (3, 0, features), (4, 0, 0)]
    pieces += [(5, 0, features * i) for i in range(4)] + [(6, shard_rows * i, 0) for i in range(4)]
    all_w = pack(
        pieces,
        [w_self_qkv, w_self_out, w_cross_q, w_cross_kv, w_cross_out, w_up, w_down],
        shard_rows,
        features,
    )
    all_w = lax.all_gather(all_w, "dp", axis=1, tiled=True)
    qkv_w = all_w[:3]
    sout_w, cq_w, ck_w, cv_w, cout_w = (all_w[3 + i] for i in range(5))
    up_ws = [all_w[8 + i] for i in range(4)]
    down_w = all_w[12:].reshape(4, examples, -1, features).transpose(1, 0, 2, 3)
    down_w = down_w.reshape(4 * features, features)
    pixels, got_blocks, earlier, prefix_other = gather_many(
        [],
        [patches[0]],
        [stem_weight_blocks(w_conv, w_patch, norm_params, s_index)],
        [captions[0], prefix[0]],
        0,
    )

    convs, patch_w, norms_low = stem_weights(got_blocks, w_conv, w_patch, norm_params)
    norms = norms_low.astype(jnp.float32)
    own_gb = own_columns(norms[:6])
    own_cells = patches.shape[1]
    number = own_cells * examples * halves
    cells = -(-number // CHUNK) * CHUNK
    rows_own = PORTIONS * GROUP
    grid = halves * own_cells
    masks = jnp.asarray(tap_masks(cells, examples))
    def to_channels(by_row, cid):
        blocks = slots_to_devices(by_row.T.reshape(PORTIONS, 32, GROUP, by_row.shape[0]))
        return exchange_all(blocks.reshape(32, rows_own, by_row.shape[0]), cid)

    def laid_out(blocks):
        flat = blocks.transpose(1, 0, 2).reshape(rows_own, number)
        return jnp.pad(flat, ((0, 0), (0, cells - number)))

    n1, r1, y1, x1 = first_block(pixels, patch_w, own_gb, masks, number)
    (x1_all,) = gather_many([x1], [], [], [], 2)
    x1_all = x1_all.reshape(features, cells)
    n2, r2, y2, x2 = conv_block(1, x1_all, convs[0], own_gb, masks, y1, number)
    inputs = captions[0].astype(jnp.float32)
    row_count = inputs.shape[0]
    earlier = earlier.astype(jnp.float32)
    low_one = layer_norm(inputs, norms[6], norms[7]).astype(LOW)
    low_all = jnp.concatenate(
        [layer_norm(earlier, norms[6], norms[7]).astype(LOW), low_one], 0
    )
    queries = (dot_float(low_one, qkv_w[0]).astype(LOW) * score_scale).astype(LOW)
    all_keys, all_values = low_dot(low_all, qkv_w[1]), low_dot(low_all, qkv_w[2])
    info = jnp.stack([s_index, caption_len[0] - s_index * row_count]).astype(jnp.int32)
    no_ok = jnp.zeros((8, 128), jnp.float32)
    self_low, self_lse, x2_all = attend_gather(info, no_ok, queries, all_keys, all_values, x2, 3)
    x2_all = x2_all.reshape(features, cells)
    n3, r3, y3, x3 = conv_block(2, x2_all, convs[1], own_gb, masks, y2, number)
    out_blocks = x3.reshape(rows_own, cells)[:, :number].reshape(rows_own, examples, grid)
    out_blocks = jnp.broadcast_to(
        out_blocks.transpose(1, 0, 2)[:, None], (examples, halves, rows_own, grid)
    )
    in_blocks = exchange_all(out_blocks.reshape(32, rows_own, grid), 4)
    patch_all = devices_to_slots(in_blocks.reshape(32, PORTIONS, GROUP, grid))
    patch_all = patch_all.reshape(features, grid).T

    prefix_own = prefix[0]
    prefix_half = prefix_own.shape[0]
    first_half = s_index == 0
    prefix_all = jnp.concatenate(
        [
            jnp.where(first_half, prefix_own, prefix_other),
            jnp.where(first_half, prefix_other, prefix_own),
        ],
        0,
    )
    memory = jnp.concatenate([prefix_all, patch_all], 0)
    mem_rows = memory.shape[0]
    prefix_total = prefix_all.shape[0]
    mem_padded = jnp.pad(memory, ((0, -mem_rows % 128), (0, 0)))
    mem_keys = low_dot(mem_padded, ck_w)
    mem_values = low_dot(mem_padded, cv_w)
    slot_ids = jnp.arange(mem_padded.shape[0], dtype=jnp.int32)
    mem_ok = (slot_ids < mem_rows) & ((slot_ids >= prefix_total) | (slot_ids < prefix_count[0]))
    mem_ok = jnp.broadcast_to(mem_ok.astype(jnp.float32)[:, None], (mem_padded.shape[0], 128))

    after_self = inputs + dot_float(self_low, sout_w)
    low_two = layer_norm(after_self, norms[8], norms[9]).astype(LOW)
    cross_q = (dot_float(low_two, cq_w).astype(LOW) * score_scale).astype(LOW)
    cross_low, cross_lse = attend("cross", info, mem_ok, cross_q, mem_keys, mem_values)
    after_cross = after_self + dot_float(cross_low, cout_w)
    low_three = layer_norm(after_cross, norms[10], norms[11]).astype(LOW)
    up_proj = jnp.concatenate([dot_float(low_three, w) for w in up_ws], 1)
    hidden = jax.nn.gelu(up_proj).astype(LOW)
    result = after_cross + dot_float(hidden, down_w)

    out_grad = cotangent[0].astype(jnp.float32)
    grad_low = cotangent[0]
    d_upper = (dot_t(grad_low, down_w) * gelu_slope(up_proj)).astype(LOW)
    d_normed = sum(dot_t(d, w) for d, w in zip(chunks(d_upper), up_ws))
    unused_three, norm_back_three = jax.vjp(layer_norm, after_cross, norms[10], norms[11])
    d_three, grad_gain_three, grad_bias_three = norm_back_three(d_normed)
    jobs = [(0, 1, row_count, 0, features * q, 0) for q in range(4)]
    jobs += [(2, 3, row_count, 0, 0, features * j) for j in range(4)]
    mlp_parts = weight_grads(
        jobs, range(8), "mlp", [hidden, grad_low, low_three, d_upper], features, row_count
    )
    mlp_parts, d_three = lax.optimization_barrier((mlp_parts, d_three))

    def scattered(parts):
        parts = parts.reshape(examples, -1, features)
        return lax.psum_scatter(parts, "dp", scatter_dimension=0, tiled=True)[0]

    def summed(own):
        other = lax.ppermute(own, "seq", [(0, 1), (1, 0)])
        return own.astype(jnp.float32) + other.astype(jnp.float32)

    mlp_own = scattered(mlp_parts)
    d_after_cross = out_grad + d_three
    cross_grad_low = d_after_cross.astype(LOW)
    d_cross = dot_t(cross_grad_low, cout_w).astype(LOW)
    d_cross_low, d_mem_keys, d_mem_values = attend_grads(
        "cross", info, mem_ok, cross_q, mem_keys, mem_values, d_cross, cross_lse, score_scale
    )
    unused_two, norm_back_two = jax.vjp(layer_norm, after_self, norms[8], norms[9])
    d_two, grad_gain_two, grad_bias_two = norm_back_two(dot_t(d_cross_low, cq_w))
    d_after_self = d_after_cross + d_two
    d_mem_rows = dot_t(d_mem_keys[:mem_rows], ck_w) + dot_t(d_mem_values[:mem_rows], cv_w)
    d_prefix = d_mem_rows[:prefix_total].reshape(halves, prefix_half, features)
    prefix_back = lax.dynamic_index_in_dim(d_prefix, s_index, 0, keepdims=False)
    away = lax.dynamic_index_in_dim(d_prefix, 1 - s_index, 0, keepdims=False).astype(LOW)
    prefix_back = prefix_back + lax.ppermute(away, "seq", [(0, 1), (1, 0)]).astype(jnp.float32)
    d_third = d_mem_rows[prefix_total:].astype(LOW)

    self_grad_low = d_after_self.astype(LOW)
    d_self = dot_t(self_grad_low, sout_w).astype(LOW)
    d_query, d_all_keys, d_all_values = attend_grads(
        "self", info, no_ok, queries, all_keys, all_values, d_self, self_lse, score_scale
    )
    d_normed_all = dot_t(d_all_keys, qkv_w[1]) + dot_t(d_all_values, qkv_w[2])
    from_later = lax.ppermute(d_normed_all[:row_count].astype(LOW), "seq", [(1, 0)])
    d_normed_one = dot_t(d_query, qkv_w[0]) + d_normed_all[row_count:]
    d_normed_one = d_normed_one + from_later.astype(jnp.float32)
    unused_one, norm_back_one = jax.vjp(layer_norm, inputs, norms[6], norms[7])
    d_one, grad_gain_one, grad_bias_one = norm_back_one(d_normed_one)
    d_inputs = d_after_self + d_one
    arrays = [cross_low, cross_grad_low, low_two, d_cross_low, mem_padded, d_mem_keys, d_mem_values]
    arrays += [self_low, self_grad_low, low_all, d_query, d_all_keys, d_all_values, low_one]
    mem_count = mem_padded.shape[0]
    jobs = [
        (0, 1, row_count, 0, 0, 0),
        (2, 3, row_count, 0, 0, 0),
        (4, 5, mem_count, 0, 0, 0),
        (4, 6, mem_count, 0, 0, 0),
        (7, 8, row_count, 0, 0, 0),
        (13, 10, row_count, 0, 0, 0),
        (9, 11, row_count, 0, 0, 0),
        (9, 11, row_count, row_count, 0, 0),
        (9, 12, row_count, 0, 0, 0),
        (9, 12, row_count, row_count, 0, 0),
    ]
    rest_parts = weight_grads(
        jobs, (0, 1, 2, 3, 4, 5, 6, 6, 7, 7), "rest", arrays, features, row_count
    )
    rest_own = scattered(rest_parts)

    d_y3 = to_channels(d_third, 6).astype(jnp.float32)
    d_y3 = laid_out(jnp.sum(d_y3.reshape(examples, halves, rows_own, grid), 1))

    def back_through(layer, d_y, n, r, x_all, w, cid):
        dx, grad_w, sums = conv_block_back(layer, d_y, n, r, own_gb, masks, x_all, w.T, number)
        total = reduce_all(dx.reshape(PORTIONS, 32, GROUP, cells), cid)
        grad_w = grad_w.reshape(9, rows_own, features).transpose(1, 0, 2)
        grad_w = grad_w.reshape(rows_own, examples, -1).transpose(1, 0, 2)
        return d_y + total.reshape(rows_own, cells), grad_w, sums

    d_y2, grad_conv_one, sums3 = back_through(2, d_y3, n3, r3, x2_all, convs[1], 7)
    d_y2, mlp_own = lax.optimization_barrier((d_y2, mlp_own))
    d_y1, grad_conv_zero, sums2 = back_through(1, d_y2, n2, r2, x1_all, convs[0], 8)
    grad_patch, sums1 = first_block_back(d_y1, n1, r1, own_gb, pixels, number)
    grad_patch = grad_patch.reshape(rows_own, examples, -1).transpose(1, 0, 2)
    patch_rows = grad_patch.shape[2]
    bn_grads = jnp.concatenate([sums1[:, :2], sums2[:, :2], sums3[:, :2]], 1).astype(LOW)
    ln_grads = jnp.stack(
        [
            grad_gain_one,
            grad_bias_one,
            grad_gain_two,
            grad_bias_two,
            grad_gain_three,
            grad_bias_three,
        ]
    ).astype(LOW)
    ln_count = ln_grads.shape[0]
    ln_blocks = ln_grads.reshape(ln_count, examples, -1).transpose(1, 0, 2)
    ln_blocks = jnp.pad(ln_blocks, ((0, 0), (0, rows_own - ln_count), (0, 0)))
    send_blocks = jnp.concatenate(
        [
            grad_conv_zero,
            grad_conv_one,
            grad_patch,
            jnp.broadcast_to(bn_grads, (examples,) + bn_grads.shape),
            ln_blocks,
        ],
        2,
    )
    got = swap_both(send_blocks, 9)
    got = got.transpose(1, 0, 2, 3).reshape(32, rows_own, -1)
    conv_rows = w_conv.shape[1]
    width = 2 * conv_rows + patch_rows
    mixed = devices_to_slots(got[:, :, : width + 6].reshape(32, PORTIONS, GROUP, width + 6))
    mixed = mixed.reshape(features, width + 6)
    stem_grads = mixed[:, :width].T.astype(jnp.float32)
    bn_part = lax.dynamic_slice_in_dim(mixed[:, width:], a_index * patch_rows, patch_rows, 0)
    ln_part = jnp.sum(got[:, :ln_count, width + 6 :].astype(jnp.float32), 0)
    norm_grads = jnp.concatenate([bn_part.T.astype(jnp.float32), ln_part], 0)

    mlp_sum, rest_sum = summed(mlp_own), summed(rest_own)
    down_sum = mlp_sum[: 4 * shard_rows]
    up_sum = [mlp_sum[(4 + i) * shard_rows : (5 + i) * shard_rows] for i in range(4)]
    rest = [rest_sum[i * shard_rows : (i + 1) * shard_rows] for i in range(8)]
    return (
        result[None].astype(LOW),
        d_inputs[None].astype(LOW),
        prefix_back[None].astype(LOW),
        stem_grads[2 * conv_rows :],
        stem_grads[: 2 * conv_rows].reshape(w_conv.shape),
        jnp.concatenate(rest[5:], 1),
        rest[4],
        rest[1],
        jnp.concatenate(rest[2:4], 1),
        rest[0],
        jnp.concatenate(up_sum, 1),
        down_sum,
        norm_grads,
    )


def suits(mesh):
    return mesh.shape["dp"] == 16 and mesh.shape["seq"] == 2


def solution(mesh):
    return jax.shard_map(
        fast_device if suits(mesh) else general_device,
        mesh=mesh,
        in_specs=(
            P("dp", "seq", None),
            P("dp", "seq", None),
            P("dp", "seq", None),
            P("dp"),
            P("dp"),
            P("dp", "seq", None),
            P("dp", None),
            P(None, "dp", None),
            P("dp", None),
            P("dp", None),
            P("dp", None),
            P("dp", None),
            P("dp", None),
            P("dp", None),
            P("dp", None),
            P(None, "dp"),
        ),
        out_specs=(
            P("dp", "seq", None),
            P("dp", "seq", None),
            P("dp", "seq", None),
            P("dp", None),
            P(None, "dp", None),
            P("dp", None),
            P("dp", None),
            P("dp", None),
            P("dp", None),
            P("dp", None),
            P("dp", None),
            P("dp", None),
            P(None, "dp"),
        ),
        check_vma=False,
    )
```

profile of v0, /device:TPU:0, one launch (start us, length us, event | category | flops | bytes accessed | tf_op | source)
XLA Modules:
  0.0 614.6 jit_solution(9468379580177659626)
XLA Ops:
  14.2 81.1 %gather_many.2 = (bf16[32,98,768]{2,1,0:T(8,128)(2,1)}, bf16[16,24,960]{2,1,0:T(8,128)(2,1)}, bf16[512,768]{1,0:T(8,128)(2,1)}, bf16[16,768]{1,0:T(8,128)(2,1)}) custom-call(bf16[98,768]{1,0:T(8,128)(2,1)} %bitcast.349, bf16[16,24,960]{2,1,0:T(8,128)(2,1)} %pad_maximum_fusion.4.refs_1_, bf16[512,768]{1,0:T(8,128)(2,1)} %bitcast.287, bf16[16,768]{1,0:T(8,128)(2,1)} %bitcast.351), custom_call_target="tpu_custom_call" | custom-call | tf_op jit(solution)/shard_map/gather_many/pallas_call | solution.py:274
  109.8 52.6 %gather_many.3 = bf16[3,32,8,3200]{3,2,1,0:T(8,128)(2,1)} custom-call(bf16[3,8,3200]{2,1,0:T(8,128)(2,1)} %copy-done.21), custom_call_target="tpu_custom_call" | custom-call | tf_op jit(solution)/shard_map/gather_many/pallas_call | solution.py:274
  162.4 4.6 stem_conv.2
  178.5 2.9 convolution_convert_fusion.1.refs_3_.k_ref
  181.4 3.2 convolution_convert_fusion.refs_4_.v_ref
  184.7 38.9 %attend_gather.1 = (bf16[512,768]{1,0:T(8,128)(2,1)S(1)}, f32[6,8,512]{2,1,0:T(8,128)S(1)}, bf16[3,32,8,3200]{3,2,1,0:T(8,128)(2,1)}) custom-call(s32[2]{0:T(128)S(1)} %pad_add_fusion.refs_0_.info_ref, f32[8,128]{1,0:T(8,128)S(1)} %broadcast_in_dim.22.refs_1_.ok_ref, bf16[512,768]{1,0:T(8,128)(2,1)S(1)} %fusion.29.refs_2_.q_ref, ...), custom_call_target="tpu_custom_call" | custom-call | tf_op jit(solution)/shard_map/attend_gather/pallas_call | solution.py:306
  223.6 5.4 stem_conv.3
  230.5 9.9 %exchange_all.2 = bf16[32,24,196]{2,1,0:T(8,128)(2,1)} custom-call(bf16[32,24,196]{2,1,0:T(8,128)(2,1)} %bitcast.325), custom_call_target="tpu_custom_call" | custom-call | tf_op jit(solution)/shard_map/exchange_all/pallas_call | solution.py:502
  251.4 6.8 %cross_attend.1 = (bf16[512,768]{1,0:T(8,128)(2,1)S(1)}, f32[6,8,512]{2,1,0:T(8,128)S(1)}) custom-call(s32[2]{0:T(128)S(1)} %pad_add_fusion.refs_0_.info_ref, f32[256,128]{1,0:T(8,128)S(1)} %broadcast_in_dim.24.ok_ref, bf16[512,768]{1,0:T(8,128)(2,1)S(1)} %fusion.30.q_ref, bf16[256,768]{1,0:T(8,128)(2,1)S(1)} %convolution_convert_fusion.7.k_ref, ...), custom_call_target="tpu_custom_call" | custom-call | flops 402653184 | bytes 2359296 | tf_op jit(solution)/shard_map/cross_attend/pallas_call | solution.py:1298
  271.8 6.3 %fusion.9.refs_3_ = bf16[512,3072]{1,0:T(8,128)(2,1)S(1)} fusion(bf16[3072,768]{1,0:T(8,128)(2,1)S(1)} %bitcast.300, f32[512,768]{1,0:T(8,128)S(1)} %fusion.41, f32[512,768]{1,0:T(8,128)S(1)} %fusion.40, f32[512,768]{1,0:T(8,128)S(1)} %fusion.38, f32[512,768]{1,0:T(8,128)S(1)} %fusion.36, bf16[1,512,768]{2,1,0:T(8,128)(2,1)S(1)} %copy-done.1), kind=kOutput, calls=%fused_computation.11 | convolution fusion | flops 2448949248 | bytes 14942208 | tf_op jit(solution)/shard_map/dot_general | solution.py:1438
  278.1 3.0 fusion.39
  285.3 3.1 multiply_reduce_fusion
  290.3 15.6 %weight_grads.2 = bf16[32,192,768]{2,1,0:T(8,128)(2,1)} custom-call(bf16[512,3072]{1,0:T(8,128)(2,1)S(1)} %multiply_convert_fusion.refs_0_, bf16[512,768]{1,0:T(8,128)(2,1)S(1)} %bitcast.273, bf16[512,768]{1,0:T(8,128)(2,1)S(1)} %add_convert_fusion.2.refs_2_, bf16[512,3072]{1,0:T(8,128)(2,1)} %copy-done.60), custom_call_target="tpu_custom_call" | custom-call | flops 4831838208 | bytes 9437184 | tf_op jit(solution)/shard_map/weight_grads/pallas_call | solution.py:1412
  306.0 2.8 pad_maximum_fusion.2.refs_9_
  311.3 8.1 %cross_attend_back.1 = (bf16[512,768]{1,0:T(8,128)(2,1)S(1)}, bf16[256,768]{1,0:T(8,128)(2,1)S(1)}, bf16[256,768]{1,0:T(8,128)(2,1)S(1)}) custom-call(s32[2]{0:T(128)S(1)} %pad_add_fusion.refs_0_.info_ref, f32[256,128]{1,0:T(8,128)S(1)} %broadcast_in_dim.24.ok_ref, bf16[512,768]{1,0:T(8,128)(2,1)S(1)} %copy-done.33, bf16[256,768]{1,0:T(8,128)(2,1)S(1)} %copy-done.35, ...), custom_call_target="tpu_custom_call" | custom-call | flops 1006632960 | bytes 4718592 | tf_op jit(solution)/shard_map/cross_attend_back/pallas_call | solution.py:1324
  319.6 2.8 multiply_reduce_fusion.1
  326.5 22.5 %self_attend_back.1 = (bf16[512,768]{1,0:T(8,128)(2,1)S(1)}, bf16[1024,768]{1,0:T(8,128)(2,1)S(1)}, bf16[1024,768]{1,0:T(8,128)(2,1)S(1)}) custom-call(s32[2]{0:T(128)S(1)} %pad_add_fusion.refs_0_.info_ref, f32[8,128]{1,0:T(8,128)S(1)} %broadcast_in_dim.22.refs_1_.ok_ref, bf16[512,768]{1,0:T(8,128)(2,1)S(1)} %copy-done.12, bf16[1024,768]{1,0:T(8,128)(2,1)} %copy-done.7, ...), custom_call_target="tpu_custom_call" | custom-call | flops 4026531840 | bytes 11796480 | tf_op jit(solution)/shard_map/self_attend_back/pallas_call | solution.py:1324
  352.3 19.9 %weight_grads.3 = bf16[32,192,768]{2,1,0:T(8,128)(2,1)} custom-call(bf16[512,768]{1,0:T(8,128)(2,1)S(1)} %get-tuple-element.62.refs_0_, bf16[512,768]{1,0:T(8,128)(2,1)S(1)} %fusion.31.refs_1_, bf16[512,768]{1,0:T(8,128)(2,1)S(1)} %add_convert_fusion.3.refs_2_, bf16[512,768]{1,0:T(8,128)(2,1)S(1)} %get-tuple-element.65.refs_3_, ...), custom_call_target="tpu_custom_call" | custom-call | flops 6039797760 | bytes 9437184 | tf_op jit(solution)/shard_map/weight_grads/pallas_call | solution.py:1412
  378.6 14.6 %exchange_all.3 = bf16[32,24,196]{2,1,0:T(8,128)(2,1)} custom-call(bf16[32,24,196]{2,1,0:T(8,128)(2,1)} %copy_bitcast_fusion.4.x_ref), custom_call_target="tpu_custom_call" | custom-call | tf_op jit(solution)/shard_map/exchange_all/pallas_call | solution.py:502
  396.5 7.5 %stem_conv_back.2 = (bf16[768,3200]{1,0:T(8,128)(2,1)}, bf16[216,768]{1,0:T(8,128)(2,1)S(1)}, f32[24,128]{1,0:T(8,128)S(1)}) custom-call(f32[24,3200]{1,0:T(8,128)S(1)} %pad.23.dy_ref, f32[24,3200]{1,0:T(8,128)S(1)} %copy-done.20, f32[24,128]{1,0:T(8,128)S(1)} %get-tuple-element.73.rstd_ref, f32[24,128]{1,0:T(8,128)S(1)} %pad.21.gb_ref, ...), custom_call_target="tpu_custom_call" | custom-call | tf_op jit(solution)/shard_map/stem_conv_back/pallas_call | solution.py:703
  406.4 42.2 %reduce_all.2 = f32[3,8,3200]{2,1,0:T(8,128)S(1)} custom-call(bf16[3,32,8,3200]{3,2,1,0:T(8,128)(2,1)S(1)} %bitcast.274), custom_call_target="tpu_custom_call" | custom-call | tf_op jit(solution)/shard_map/reduce_all/pallas_call | solution.py:396
  448.7 3.0 fusion.32
  451.7 3.0 convolution_add_fusion
  457.5 3.5 fusion.28
  462.2 2.8 reshape.365
  467.7 9.5 %collective-permute-done = bf16[512,768]{1,0:T(8,128)(2,1)} collective-permute-done((bf16[512,768]{1,0:T(8,128)(2,1)}, bf16[512,768]{1,0:T(8,128)(2,1)}, u32[]{:S(2)}, u32[]{:S(2)}) %collective-permute-start) | collective-permute-done | bytes 786464 | tf_op jit(solution)/shard_map/ppermute | solution.py:1649
  477.2 3.2 fusion.72
  481.8 4.3 fusion.44
  486.2 7.8 %stem_conv_back.3 = (bf16[768,3200]{1,0:T(8,128)(2,1)}, bf16[216,768]{1,0:T(8,128)(2,1)S(1)}, f32[24,128]{1,0:T(8,128)S(1)}) custom-call(f32[24,3200]{1,0:T(8,128)S(1)} %bitcast_add_fusion.1.dy_ref, f32[24,3200]{1,0:T(8,128)S(1)} %copy-done.18, f32[24,128]{1,0:T(8,128)S(1)} %get-tuple-element.78.rstd_ref, f32[24,128]{1,0:T(8,128)S(1)} %pad.21.gb_ref, ...), custom_call_target="tpu_custom_call" | custom-call | tf_op jit(solution)/shard_map/stem_conv_back/pallas_call | solution.py:703
  496.4 47.3 %reduce_all.3 = f32[3,8,3200]{2,1,0:T(8,128)S(1)} custom-call(bf16[3,32,8,3200]{3,2,1,0:T(8,128)(2,1)S(1)} %bitcast.275), custom_call_target="tpu_custom_call" | custom-call | tf_op jit(solution)/shard_map/reduce_all/pallas_call | solution.py:396
  548.4 35.5 %swap_both.1 = bf16[2,16,24,966]{3,2,1,0:T(8,128)(2,1)} custom-call(bf16[16,24,966]{2,1,0:T(8,128)(2,1)} %concatenate.46.x_ref), custom_call_target="tpu_custom_call" | custom-call | tf_op jit(solution)/shard_map/swap_both/pallas_call | solution.py:458
  595.2 8.2 %collective-permute-done.2 = bf16[384,768]{1,0:T(8,128)(2,1)} collective-permute-done((bf16[384,768]{1,0:T(8,128)(2,1)}, bf16[384,768]{1,0:T(8,128)(2,1)}, u32[]{:S(2)}, u32[]{:S(2)}) %collective-permute-start.2) | collective-permute-done | bytes 589856 | tf_op jit(solution)/shard_map/ppermute | solution.py:1623
  (376 shorter events, 115.4 us)
Async XLA Ops:
  7.2 163.9 %all-gather.2.cloned.1.call-start = ((), (), s32[]{:S(2)}) async-start(), calls=%async_computation.2 | async-start | bytes 20054016 | tf_op jit(solution)/shard_map/all_gather | solution.py:1518
  9.8 476.4 %reduce-scatter.3.cloned.1.call-start = ((), (), s32[]{:S(2)}) async-start(), calls=%async_computation.3 | async-start | bytes 10027008 | tf_op jit(solution)/shard_map/reduce_scatter | solution.py:1620
  169.3 77.6 %copy-start.61 = (bf16[16,768]{1,0:T(8,128)(2,1)}, bf16[16,768]{1,0:T(8,128)(2,1)S(1)}, u32[]{:S(2)}) copy-start(bf16[16,768]{1,0:T(8,128)(2,1)S(1)} %get-tuple-element.190) | copy-start | bytes 73732
  169.3 77.6 %copy-start.63 = (bf16[16,768]{1,0:T(8,128)(2,1)}, bf16[16,768]{1,0:T(8,128)(2,1)S(1)}, u32[]{:S(2)}) copy-start(bf16[16,768]{1,0:T(8,128)(2,1)S(1)} %get-tuple-element.191) | copy-start | bytes 73732
  184.6 38.9 %copy-start.8 = (bf16[1024,768]{1,0:T(8,128)(2,1)}, bf16[1024,768]{1,0:T(8,128)(2,1)S(1)}, u32[]{:S(2)}) copy-start(bf16[1024,768]{1,0:T(8,128)(2,1)S(1)} %convolution_convert_fusion.refs_4_.v_ref) | copy-start | bytes 4718596
  229.1 12.5 %copy-start.19 = (f32[24,3200]{1,0:T(8,128)}, f32[24,3200]{1,0:T(8,128)S(1)}, u32[]{:S(2)}) copy-start(f32[24,3200]{1,0:T(8,128)S(1)} %get-tuple-element.72.n_ref) | copy-start | bytes 921604
  244.2 14.0 %copy-start.45 = (f32[512,768]{1,0:T(8,128)}, f32[512,768]{1,0:T(8,128)S(1)}, u32[]{:S(2)}) copy-start(f32[512,768]{1,0:T(8,128)S(1)} %get-tuple-element.195) | copy-start | bytes 4718596
  251.2 9.1 %copy-start.32 = (bf16[512,768]{1,0:T(8,128)(2,1)}, bf16[512,768]{1,0:T(8,128)(2,1)S(1)}, u32[]{:S(2)}) copy-start(bf16[512,768]{1,0:T(8,128)(2,1)S(1)} %fusion.30.q_ref) | copy-start | bytes 2359300
  260.3 28.1 %copy-start.40 = (f32[512,768]{1,0:T(8,128)}, f32[512,768]{1,0:T(8,128)S(1)}, u32[]{:S(2)}) copy-start(f32[512,768]{1,0:T(8,128)S(1)} %get-tuple-element.197) | copy-start | bytes 4718596
  271.8 18.6 %copy-start.5 = (bf16[512,3072]{1,0:T(8,128)(2,1)}, bf16[512,3072]{1,0:T(8,128)(2,1)S(1)}, u32[]{:S(2)}) copy-start(bf16[512,3072]{1,0:T(8,128)(2,1)S(1)} %multiply_convert_fusion.refs_0_) | copy-start | bytes 9437188
  306.0 282.1 %reduce-scatter.5.cloned.1.call-start = ((), (), s32[]{:S(2)}) async-start(), calls=%async_computation.4 | async-start | bytes 10027008 | tf_op jit(solution)/shard_map/reduce_scatter | solution.py:1620
  311.3 8.3 %copy-start.46 = (f32[512,768]{1,0:T(8,128)S(1)}, f32[512,768]{1,0:T(8,128)}, u32[]{:S(2)}) copy-start(f32[512,768]{1,0:T(8,128)} %copy-done.45) | copy-start | bytes 4718596
  311.3 8.3 %copy-start.68 = (f32[512]{0:T(512)S(1)}, f32[512]{0:T(512)}, u32[]{:S(2)}) copy-start(f32[512]{0:T(512)} %copy-done.67) | copy-start | bytes 6148
  311.3 8.3 %copy-start.73 = (f32[512]{0:T(512)S(1)}, f32[512]{0:T(512)}, u32[]{:S(2)}) copy-start(f32[512]{0:T(512)} %copy-done.72) | copy-start | bytes 6148
  319.5 32.8 %copy-start.13 = (bf16[256,768]{1,0:T(8,128)(2,1)}, bf16[256,768]{1,0:T(8,128)(2,1)S(1)}, u32[]{:S(2)}) copy-start(bf16[256,768]{1,0:T(8,128)(2,1)S(1)} %get-tuple-element.71.refs_6_) | copy-start | bytes 1179652
  319.5 32.8 %copy-start.27 = (bf16[256,768]{1,0:T(8,128)(2,1)}, bf16[256,768]{1,0:T(8,128)(2,1)S(1)}, u32[]{:S(2)}) copy-start(bf16[256,768]{1,0:T(8,128)(2,1)S(1)} %get-tuple-element.70.refs_5_) | copy-start | bytes 1179652
  326.5 25.7 %copy-start.24 = (bf16[512,768]{1,0:T(8,128)(2,1)S(1)}, bf16[512,768]{1,0:T(8,128)(2,1)}, u32[]{:S(2)}) copy-start(bf16[512,768]{1,0:T(8,128)(2,1)} %copy-done.22) | copy-start | bytes 2359300
  376.6 90.6 %collective-permute-start.1 = (bf16[16,768]{1,0:T(8,128)(2,1)S(1)}, bf16[16,768]{1,0:T(8,128)(2,1)S(1)}, u32[]{:S(2)}, u32[]{:S(2)}) collective-permute-start(bf16[16,768]{1,0:T(8,128)(2,1)S(1)} %fusion.62), channel_id=1, source_target_pairs={{0,1},{1,0},{2,3},{3,2},{4,5},{5,4},{6,7},{7,6},{8,9},{9,8},{10,11... | collective-permute-start | bytes 73736 | tf_op jit(solution)/shard_map/ppermute | solution.py:1640
  406.4 42.2 %copy-start.29 = (bf16[1024,768]{1,0:T(8,128)(2,1)S(1)}, bf16[1024,768]{1,0:T(8,128)(2,1)}, u32[]{:S(2)}) copy-start(bf16[1024,768]{1,0:T(8,128)(2,1)} %copy-done.28) | copy-start | bytes 4718596
  406.4 51.0 %slice-start.5 = ((s8[4718592]{0:T(1024)(128)(4,1)}), s8[4194304]{0:T(1024)(128)(4,1)S(1)}, s32[]{:S(2)}) async-start(s8[4718592]{0:T(1024)(128)(4,1)} %bitcast.301), calls=%async_computation.10 | async-start | bytes 8388608
  448.7 8.8 %slice-start.6 = ((s8[4718592]{0:T(1024)(128)(4,1)}), s8[524288]{0:T(1024)(128)(4,1)S(1)}, s32[]{:S(2)}) async-start(s8[4718592]{0:T(1024)(128)(4,1)} %bitcast.301), calls=%async_computation.11 | async-start | bytes 1048576
  455.7 21.5 %collective-permute-start = (bf16[512,768]{1,0:T(8,128)(2,1)}, bf16[512,768]{1,0:T(8,128)(2,1)}, u32[]{:S(2)}, u32[]{:S(2)}) collective-permute-start(bf16[512,768]{1,0:T(8,128)(2,1)} %slice.455), channel_id=1, source_target_pairs={{1,0},{3,2},{5,4},{7,6},{9,8},{11,10},{13,12},{15,14},{17,16},{19,... | collective-permute-start | bytes 2359304 | tf_op jit(solution)/shard_map/ppermute | solution.py:1649
  461.1 16.1 %copy-start.31 = (bf16[512,768]{1,0:T(8,128)(2,1)S(1)}, bf16[512,768]{1,0:T(8,128)(2,1)}, u32[]{:S(2)}) copy-start(bf16[512,768]{1,0:T(8,128)(2,1)} %copy-done.30) | copy-start | bytes 2359300
  462.2 15.0 %copy-start.44 = (bf16[1,512,768]{2,1,0:T(8,128)(2,1)S(1)}, bf16[1,512,768]{2,1,0:T(8,128)(2,1)}, u32[]{:S(2)}) copy-start(bf16[1,512,768]{2,1,0:T(8,128)(2,1)} %param.17) | copy-start | bytes 2359300
  467.7 12.6 %copy-start.75 = (f32[512]{0:T(512)S(1)}, f32[512]{0:T(512)}, u32[]{:S(2)}) copy-start(f32[512]{0:T(512)} %copy-done.74) | copy-start | bytes 6148
  467.7 12.7 %copy-start.70 = (f32[512]{0:T(512)S(1)}, f32[512]{0:T(512)}, u32[]{:S(2)}) copy-start(f32[512]{0:T(512)} %copy-done.69) | copy-start | bytes 6148
  481.8 61.9 %slice-start = ((s8[5111808]{0:T(1024)(128)(4,1)}), s8[917504]{0:T(1024)(128)(4,1)S(1)}, s32[]{:S(2)}) async-start(s8[5111808]{0:T(1024)(128)(4,1)} %bitcast.271), calls=%async_computation.5 | async-start | bytes 1835008
  486.2 57.6 %slice-start.1 = ((s8[5111808]{0:T(1024)(128)(4,1)}), s8[4194304]{0:T(1024)(128)(4,1)S(1)}, s32[]{:S(2)}) async-start(s8[5111808]{0:T(1024)(128)(4,1)} %bitcast.271), calls=%async_computation.6 | async-start | bytes 8388608
  496.4 47.3 %copy-start.16 = (f32[24,3200]{1,0:T(8,128)S(1)}, f32[24,3200]{1,0:T(8,128)}, u32[]{:S(2)}) copy-start(f32[24,3200]{1,0:T(8,128)} %copy-done.15) | copy-start | bytes 921604
  546.9 46.1 %collective-permute-start.3 = (bf16[384,768]{1,0:T(8,128)(2,1)}, bf16[384,768]{1,0:T(8,128)(2,1)}, u32[]{:S(2)}, u32[]{:S(2)}) collective-permute-start(bf16[384,768]{1,0:T(8,128)(2,1)} %bitcast.88), channel_id=1, source_target_pairs={{0,1},{1,0},{2,3},{3,2},{4,5},{5,4},{6,7},{7,6},{8,9},{9,8},{10,11... | collective-permute-start | bytes 1769480 | tf_op jit(solution)/shard_map/ppermute | solution.py:1623
  588.1 15.4 %collective-permute-start.2 = (bf16[384,768]{1,0:T(8,128)(2,1)}, bf16[384,768]{1,0:T(8,128)(2,1)}, u32[]{:S(2)}, u32[]{:S(2)}) collective-permute-start(bf16[384,768]{1,0:T(8,128)(2,1)} %bitcast.333), channel_id=1, source_target_pairs={{0,1},{1,0},{2,3},{3,2},{4,5},{5,4},{6,7},{7,6},{8,9},{9,8},{10,11... | collective-permute-start | bytes 1769480 | tf_op jit(solution)/shard_map/ppermute | solution.py:1623
  594.3 9.2 %copy-start.59 = (bf16[1,384,768]{2,1,0:T(8,128)(2,1)S(1)}, bf16[1,384,768]{2,1,0:T(8,128)(2,1)}, u32[]{:S(2)}) copy-start(bf16[1,384,768]{2,1,0:T(8,128)(2,1)} %reduce-scatter.5.cloned.1.call-done) | copy-start | bytes 1769476
  (66 other events, 199.6 us)
Sparse Core Ops, SparseCore 0:
  10.2 152.3 all-gather.1
  306.1 121.7 reduce-scatter.2
  432.5 136.9 reduce-scatter.4
where the time goes:
time: 625 us; the launch traced here: 615 us
  Pallas kernels  426 us (68%)
  matrix products  67.4 us (11%)
  local copies, waits for them, and re-layouts  52 us (8%)
  other arithmetic  30.4 us (5%)
  waiting for transfers between devices  17.8 us (3%)
  between operations  17.4 us (3%)
    pallas_call x2, Pallas kernels, gather_many(): pl.pallas_call(functools.partial(gather_body, tuple(kinds), len(swaps), l...  134 us
    pallas_call x2, Pallas kernels, reduce_all(): pl.pallas_call(reduce_body, name='reduce_all', out_shape=jax.ShapeDtypeSt...  89.5 us
    pallas_call x1, Pallas kernels, attend_gather(): pl.pallas_call(functools.partial(attend_gather_body, width), name='attend...  38.9 us
    dot_general x13, matrix products, dot_t(): lax.dot_general(left, right, (((1,), (1,)), ((), ())), preferred_element_...  36.7 us
    pallas_call x1, Pallas kernels, swap_both(): pl.pallas_call(swap_both_body, name='swap_both', out_shape=jax.ShapeDtype...  35.5 us
    pallas_call x2, Pallas kernels, weight_grads(): pl.pallas_call(functools.partial(weight_grads_body, tuple(jobs), tuple(ta...  35.5 us
    dot_general x13, matrix products, dot_float(): return jnp.dot(left, right, preferred_element_type=jnp.float32)  30.7 us
    pallas_call x2, Pallas kernels, attend_grads(): pl.pallas_call(functools.partial(attend_back_body, kind, width, scale), n...  30.6 us
  transfers between devices with their start and end apart: 7, of which 2 were waited for; matrix products, arithmetic and copies ran while one was open for 12% of the time, Pallas kernels for 57%

commit v1 on v0

--- a/solution.py
+++ b/solution.py
@@ -340,12 +340,91 @@
     )(*arrays)
 
 
-def reduce_body(x_ref, o_ref, r0, r1, r2, r3, r4, send_sem, recv_sem):
+def swap_both_steps(x_ref, pair_ref, o_ref, other_ref, sems):
+    send_sem, recv_sem, pass_sem, got_sem, own_sem, pair_sem = sems
+    a, s = lax.axis_index("dp"), lax.axis_index("seq")
+    count = x_ref.shape[0]
+    partners = [(lax.rem(a + j, count), s) for j in range(1, count)] + [(a, 1 - s)]
+
+    def own():
+        return pltpu.make_async_copy(x_ref.at[a], o_ref.at[s, a], own_sem)
+
+    def direct(j):
+        to = lax.rem(a + j, count)
+        return pltpu.make_async_remote_copy(
+            src_ref=x_ref.at[to],
+            dst_ref=o_ref.at[s, a],
+            send_sem=send_sem.at[j],
+            recv_sem=recv_sem.at[j],
+            device_id=(to, s),
+            device_id_type=MESH,
+        )
+
+    def onward(j):
+        source = lax.rem(a - j + count, count)
+        return pltpu.make_async_remote_copy(
+            src_ref=o_ref.at[s, source] if j else x_ref.at[a],
+            dst_ref=o_ref.at[s, source],
+            send_sem=pass_sem.at[j],
+            recv_sem=got_sem.at[j],
+            device_id=(a, 1 - s),
+            device_id_type=MESH,
+        )
+
+    def paired():
+        return pltpu.make_async_remote_copy(
+            src_ref=pair_ref,
+            dst_ref=other_ref,
+            send_sem=pair_sem.at[0],
+            recv_sem=pair_sem.at[1],
+            device_id=(a, 1 - s),
+            device_id_type=MESH,
+        )
+
+    def start():
+        own().start()
+        paired().start()
+        onward(0).start()
+        for j in range(1, count):
+            direct(j).start()
+
+    def pass_on():
+        for j in range(1, count):
+            arrived(o_ref.at[s, lax.rem(a - j + count, count)], recv_sem.at[j])
+            onward(j).start()
+
+    def finish():
+        for j in range(count):
+            arrived(o_ref.at[1 - s, lax.rem(a - j + count, count)], got_sem.at[j])
+        for j in range(1, count):
+            direct(j).wait_send()
+        for j in range(count):
+            onward(j).wait_send()
+        own().wait()
+        paired().wait()
+
+    return partners, start, pass_on, finish
+
+
+def swap_both_sems(count):
+    return [pltpu.SemaphoreType.DMA((count,))] * 4 + [
+        pltpu.SemaphoreType.DMA,
+        pltpu.SemaphoreType.DMA((2,)),
+    ]
+
+
+def reduce_body(swaps, *refs):
+    count = 1 + swaps
+    ins, outs, refs = refs[:count], refs[count : 2 * count], refs[2 * count :]
+    x_ref, o_ref = ins[0], outs[0]
+    bufs, (send_sem, recv_sem) = refs[:5], refs[5:7]
     bits = my_bits()
-    greet([place(flipped(bits, b)) for b in range(5)])
+    partners = [place(flipped(bits, b)) for b in range(5)]
+    if swaps:
+        others, start, pass_on, finish = swap_both_steps(*ins[1:], *outs[1:], refs[7:])
+        partners += others
+    greet(partners)
     started = []
-    slots = [slot_of(bits, p) for p in range(PORTIONS)]
-    bufs = (r0, r1, r2, r3, r4)
 
     def send(p, src, dst, bit, k):
         copy = pltpu.make_async_remote_copy(
@@ -361,17 +440,19 @@
 
     for p in range(PORTIONS):
         away = 16 * (1 - bits[1])
-        send(p, x_ref.at[p, pl.ds(away, 16)], r0.at[p], 1, 0)
+        send(p, x_ref.at[p, pl.ds(away, 16)], bufs[0].at[p], 1, 0)
     for k in range(5):
         size = 16 >> k
+        if swaps and k == 1:
+            start()
+        if swaps and k == 4:
+            pass_on()
         for p in range(PORTIONS):
-            got = bufs[k].at[p]
-            arrived(got, recv_sem.at[p, k])
+            arrived(bufs[k].at[p], recv_sem.at[p, k])
             if k == 0:
                 base, held = 16 * bits[1], x_ref
             else:
-                bit = bits[STEPS[p][4 - k]]
-                base, held = size * bit, bufs[k - 1]
+                base, held = size * bits[STEPS[p][4 - k]], bufs[k - 1]
             if k == 4:
                 o_ref[p] = held[p, base].astype(jnp.float32) + bufs[k][p, 0].astype(jnp.float32)
                 continue
@@ -379,91 +460,63 @@
                 total = held[p, base + j].astype(jnp.float32) + bufs[k][p, j].astype(jnp.float32)
                 bufs[k][p, j] = total.astype(bufs[k].dtype)
             half = size // 2
-            nbit = bits[STEPS[p][3 - k]]
             send(
                 p,
-                bufs[k].at[p, pl.ds(half * (1 - nbit), half)],
+                bufs[k].at[p, pl.ds(half * (1 - bits[STEPS[p][3 - k]]), half)],
                 bufs[k + 1].at[p],
                 STEPS[p][3 - k],
                 k + 1,
             )
+    if swaps:
+        finish()
     for copy in started:
         copy.wait_send()
 
 
-def reduce_all(x, cid):
+def reduce_all(x, swaps, cid):
     rest = x.shape[2:]
+    vmem, hbm = pl.BlockSpec(memory_space=pltpu.VMEM), pl.BlockSpec(memory_space=pltpu.HBM)
     return pl.pallas_call(
-        reduce_body,
+        functools.partial(reduce_body, len(swaps)),
         name="reduce_all",
-        out_shape=jax.ShapeDtypeStruct((PORTIONS,) + rest, jnp.float32),
-        in_specs=[pl.BlockSpec(memory_space=pltpu.VMEM)],
-        out_specs=pl.BlockSpec(memory_space=pltpu.VMEM),
+        out_shape=tuple(
+            [jax.ShapeDtypeStruct((PORTIONS,) + rest, jnp.float32)]
+            + [jax.ShapeDtypeStruct((2,) + g.shape, g.dtype) for g in swaps[:1]]
+            + [jax.ShapeDtypeStruct(g.shape, g.dtype) for g in swaps[1:]]
+        ),
+        in_specs=[vmem] + [hbm] * len(swaps),
+        out_specs=tuple([vmem] + [hbm] * len(swaps)),
         scratch_shapes=[pltpu.VMEM((PORTIONS, 16 >> k) + rest, x.dtype) for k in range(5)]
-        + [pltpu.SemaphoreType.DMA((PORTIONS, 5)), pltpu.SemaphoreType.DMA((PORTIONS, 5))],
+        + [pltpu.SemaphoreType.DMA((PORTIONS, 5)), pltpu.SemaphoreType.DMA((PORTIONS, 5))]
+        + (swap_both_sems(swaps[0].shape[0]) if swaps else []),
         compiler_params=pltpu.CompilerParams(
             collective_id=cid, has_side_effects=True, vmem_limit_bytes=40 << 20
         ),
-    )(x)
-
-
-def swap_both_body(x_ref, o_ref, send_sem, recv_sem, pass_sem, got_sem, own_sem):
-    a, s = lax.axis_index("dp"), lax.axis_index("seq")
-    count = x_ref.shape[0]
-    greet([(lax.rem(a + j, count), s) for j in range(1, count)] + [(a, 1 - s)])
-    own = pltpu.make_async_copy(x_ref.at[a], o_ref.at[s, a], own_sem)
-    own.start()
-    copies = []
-
-    def pass_on(src, slot, j):
-        copy = pltpu.make_async_remote_copy(
-            src_ref=src,
-            dst_ref=o_ref.at[s, slot],
-            send_sem=pass_sem.at[j],
-            recv_sem=got_sem.at[j],
-            device_id=(a, 1 - s),
-            device_id_type=MESH,
-        )
-        copy.start()
-        copies.append(copy)
-
-    pass_on(x_ref.at[a], a, 0)
-    for j in range(1, count):
-        to = lax.rem(a + j, count)
-        copy = pltpu.make_async_remote_copy(
-            src_ref=x_ref.at[to],
-            dst_ref=o_ref.at[s, a],
-            send_sem=send_sem.at[j],
-            recv_sem=recv_sem.at[j],
-            device_id=(to, s),
-            device_id_type=MESH,
-        )
-        copy.start()
-        copies.append(copy)
-    for j in range(1, count):
-        source = lax.rem(a - j + count, count)
-        got = o_ref.at[s, source]
-        arrived(got, recv_sem.at[j])
-        pass_on(got, source, j)
-    for j in range(count):
-        got = o_ref.at[1 - s, lax.rem(a - j + count, count)]
-        arrived(got, got_sem.at[j])
-    for copy in copies:
-        copy.wait_send()
-    own.wait()
-
-
-def swap_both(x, cid):
-    count = x.shape[0]
+    )(x, *swaps)
+
+
+def swap_both_body(x_ref, pair_ref, o_ref, other_ref, *sems):
+    partners, start, pass_on, finish = swap_both_steps(x_ref, pair_ref, o_ref, other_ref, sems)
+    greet(partners)
+    start()
+    pass_on()
+    finish()
+
+
+def swap_both(x, pair, cid):
+    space = pl.BlockSpec(memory_space=pltpu.HBM)
     return pl.pallas_call(
         swap_both_body,
         name="swap_both",
-        out_shape=jax.ShapeDtypeStruct((2,) + x.shape, x.dtype),
-        in_specs=[pl.BlockSpec(memory_space=pltpu.HBM)],
-        out_specs=pl.BlockSpec(memory_space=pltpu.HBM),
-        scratch_shapes=[pltpu.SemaphoreType.DMA((count,))] * 4 + [pltpu.SemaphoreType.DMA],
+        out_shape=(
+            jax.ShapeDtypeStruct((2,) + x.shape, x.dtype),
+            jax.ShapeDtypeStruct(pair.shape, pair.dtype),
+        ),
+        in_specs=[space] * 2,
+        out_specs=(space,) * 2,
+        scratch_shapes=swap_both_sems(x.shape[0]),
         compiler_params=pltpu.CompilerParams(collective_id=cid, has_side_effects=True),
-    )(x)
+    )(x, pair)
 
 
 def exchange_body(x_ref, o_ref, send_sem, recv_sem, own_sem):
@@ -1605,23 +1658,19 @@
     out_grad = cotangent[0].astype(jnp.float32)
     grad_low = cotangent[0]
     d_upper = (dot_t(grad_low, down_w) * gelu_slope(up_proj)).astype(LOW)
-    d_normed = sum(dot_t(d, w) for d, w in zip(chunks(d_upper), up_ws))
-    unused_three, norm_back_three = jax.vjp(layer_norm, after_cross, norms[10], norms[11])
-    d_three, grad_gain_three, grad_bias_three = norm_back_three(d_normed)
     jobs = [(0, 1, row_count, 0, features * q, 0) for q in range(4)]
     jobs += [(2, 3, row_count, 0, 0, features * j) for j in range(4)]
     mlp_parts = weight_grads(
         jobs, range(8), "mlp", [hidden, grad_low, low_three, d_upper], features, row_count
     )
-    mlp_parts, d_three = lax.optimization_barrier((mlp_parts, d_three))
+    mlp_parts, d_upper = lax.optimization_barrier((mlp_parts, d_upper))
+    d_normed = sum(dot_t(d, w) for d, w in zip(chunks(d_upper), up_ws))
+    unused_three, norm_back_three = jax.vjp(layer_norm, after_cross, norms[10], norms[11])
+    d_three, grad_gain_three, grad_bias_three = norm_back_three(d_normed)
 
     def scattered(parts):
         parts = parts.reshape(examples, -1, features)
         return lax.psum_scatter(parts, "dp", scatter_dimension=0, tiled=True)[0]
-
-    def summed(own):
-        other = lax.ppermute(own, "seq", [(0, 1), (1, 0)])
-        return own.astype(jnp.float32) + other.astype(jnp.float32)
 
     mlp_own = scattered(mlp_parts)
     d_after_cross = out_grad + d_three
@@ -1637,7 +1686,6 @@
     d_prefix = d_mem_rows[:prefix_total].reshape(halves, prefix_half, features)
     prefix_back = lax.dynamic_index_in_dim(d_prefix, s_index, 0, keepdims=False)
     away = lax.dynamic_index_in_dim(d_prefix, 1 - s_index, 0, keepdims=False).astype(LOW)
-    prefix_back = prefix_back + lax.ppermute(away, "seq", [(0, 1), (1, 0)]).astype(jnp.float32)
     d_third = d_mem_rows[prefix_total:].astype(LOW)
 
     self_grad_low = d_after_self.astype(LOW)
@@ -1647,11 +1695,6 @@
     )
     d_normed_all = dot_t(d_all_keys, qkv_w[1]) + dot_t(d_all_values, qkv_w[2])
     from_later = lax.ppermute(d_normed_all[:row_count].astype(LOW), "seq", [(1, 0)])
-    d_normed_one = dot_t(d_query, qkv_w[0]) + d_normed_all[row_count:]
-    d_normed_one = d_normed_one + from_later.astype(jnp.float32)
-    unused_one, norm_back_one = jax.vjp(layer_norm, inputs, norms[6], norms[7])
-    d_one, grad_gain_one, grad_bias_one = norm_back_one(d_normed_one)
-    d_inputs = d_after_self + d_one
     arrays = [cross_low, cross_grad_low, low_two, d_cross_low, mem_padded, d_mem_keys, d_mem_values]
     arrays += [self_low, self_grad_low, low_all, d_query, d_all_keys, d_all_values, low_one]
     mem_count = mem_padded.shape[0]
@@ -1675,16 +1718,26 @@
     d_y3 = to_channels(d_third, 6).astype(jnp.float32)
     d_y3 = laid_out(jnp.sum(d_y3.reshape(examples, halves, rows_own, grid), 1))
 
-    def back_through(layer, d_y, n, r, x_all, w, cid):
+    def back_through(layer, d_y, n, r, x_all, w, swaps, cid):
         dx, grad_w, sums = conv_block_back(layer, d_y, n, r, own_gb, masks, x_all, w.T, number)
-        total = reduce_all(dx.reshape(PORTIONS, 32, GROUP, cells), cid)
+        total, *got = reduce_all(dx.reshape(PORTIONS, 32, GROUP, cells), swaps, cid)
         grad_w = grad_w.reshape(9, rows_own, features).transpose(1, 0, 2)
         grad_w = grad_w.reshape(rows_own, examples, -1).transpose(1, 0, 2)
-        return d_y + total.reshape(rows_own, cells), grad_w, sums
-
-    d_y2, grad_conv_one, sums3 = back_through(2, d_y3, n3, r3, x2_all, convs[1], 7)
+        return d_y + total.reshape(rows_own, cells), grad_w, sums, got
+
+    d_y2, grad_conv_one, sums3, _ = back_through(2, d_y3, n3, r3, x2_all, convs[1], [], 7)
     d_y2, mlp_own = lax.optimization_barrier((d_y2, mlp_own))
-    d_y1, grad_conv_zero, sums2 = back_through(1, d_y2, n2, r2, x1_all, convs[0], 8)
+    d_y1, grad_conv_zero, sums2, got = back_through(
+        1, d_y2, n2, r2, x1_all, convs[0], [grad_conv_one, away], 8
+    )
+    got_one, prefix_part = got
+    prefix_back = prefix_back + prefix_part.astype(jnp.float32)
+    from_later, d_y1 = lax.optimization_barrier((from_later, d_y1))
+    d_normed_one = dot_t(d_query, qkv_w[0]) + d_normed_all[row_count:]
+    d_normed_one = d_normed_one + from_later.astype(jnp.float32)
+    unused_one, norm_back_one = jax.vjp(layer_norm, inputs, norms[6], norms[7])
+    d_one, grad_gain_one, grad_bias_one = norm_back_one(d_normed_one)
+    d_inputs = d_after_self + d_one
     grad_patch, sums1 = first_block_back(d_y1, n1, r1, own_gb, pixels, number)
     grad_patch = grad_patch.reshape(rows_own, examples, -1).transpose(1, 0, 2)
     patch_rows = grad_patch.shape[2]
@@ -1705,25 +1758,35 @@
     send_blocks = jnp.concatenate(
         [
             grad_conv_zero,
-            grad_conv_one,
             grad_patch,
             jnp.broadcast_to(bn_grads, (examples,) + bn_grads.shape),
             ln_blocks,
         ],
         2,
     )
-    got = swap_both(send_blocks, 9)
-    got = got.transpose(1, 0, 2, 3).reshape(32, rows_own, -1)
+    def by_sender(blocks):
+        return blocks.transpose(1, 0, 2, 3).reshape(32, rows_own, -1)
+
+    def channels_last(blocks):
+        mixed = devices_to_slots(blocks.reshape(32, PORTIONS, GROUP, -1))
+        return mixed.reshape(features, -1)
+
+    mlp_other = lax.ppermute(mlp_own, "seq", [(0, 1), (1, 0)])
+    got, rest_other = swap_both(send_blocks, rest_own, 9)
+    got = by_sender(got)
+    width = w_conv.shape[1] + patch_rows
+    mixed = channels_last(got[:, :, : width + 6])
     conv_rows = w_conv.shape[1]
-    width = 2 * conv_rows + patch_rows
-    mixed = devices_to_slots(got[:, :, : width + 6].reshape(32, PORTIONS, GROUP, width + 6))
-    mixed = mixed.reshape(features, width + 6)
-    stem_grads = mixed[:, :width].T.astype(jnp.float32)
+    stem_grads = jnp.concatenate(
+        [mixed[:, :conv_rows], channels_last(by_sender(got_one)), mixed[:, conv_rows:width]], 1
+    )
+    stem_grads = stem_grads.T.astype(jnp.float32)
     bn_part = lax.dynamic_slice_in_dim(mixed[:, width:], a_index * patch_rows, patch_rows, 0)
     ln_part = jnp.sum(got[:, :ln_count, width + 6 :].astype(jnp.float32), 0)
     norm_grads = jnp.concatenate([bn_part.T.astype(jnp.float32), ln_part], 0)
 
-    mlp_sum, rest_sum = summed(mlp_own), summed(rest_own)
+    mlp_sum = mlp_own.astype(jnp.float32) + mlp_other.astype(jnp.float32)
+    rest_sum = rest_own.astype(jnp.float32) + rest_other.astype(jnp.float32)
     down_sum = mlp_sum[: 4 * shard_rows]
     up_sum = [mlp_sum[(4 + i) * shard_rows : (5 + i) * shard_rows] for i in range(4)]
     rest = [rest_sum[i * shard_rows : (i + 1) * shard_rows] for i in range(8)]

time: 625 us -> 615 us (0.984)
  waiting for transfers between devices: 17.8 us -> 1.88 us
    ppermute x1, waiting for transfers between devices: 9.47 us -> 0.01 us  [fast_device(): lax.ppermute(d_normed_all[:row_count].astype(LOW), 'seq', [(1, 0)])]
    ppermute x3 -> x1, waiting for transfers between devices: 8.25 us -> 0.01 us  [fast_device(): mlp_other = lax.ppermute(mlp_own, 'seq', [(0, 1), (1, 0)])]
    pallas_call x2, Pallas kernels: 24.5 us -> 31.7 us  [exchange_all(): pl.pallas_call(exchange_body, name='exchange_all', out_shape=jax.ShapeDty...]
    unnamed x184 -> x244, local copies, waits for them, and re-layouts: 16.8 us -> 19.2 us
  transfers between devices with their start and end apart: 7 -> 5, of which waited for: 2 -> 1; matrix products, arithmetic and copies ran while one was open for 12% -> 14% of each run, Pallas kernels for 57% -> 53%
where the time goes in v1:
time: 615 us; the launch traced here: 605 us
  Pallas kernels  431 us (70%)
  matrix products  68.4 us (11%)
  local copies, waits for them, and re-layouts  55.1 us (9%)
  other arithmetic  28 us (5%)
  between operations  17.9 us (3%)
    pallas_call x2, Pallas kernels, gather_many(): pl.pallas_call(functools.partial(gather_body, tuple(kinds), len(swaps), l...  133 us
    pallas_call x2, Pallas kernels, reduce_all(): pl.pallas_call(functools.partial(reduce_body, len(swaps)), name='reduce_a...  94.9 us
    pallas_call x1, Pallas kernels, attend_gather(): pl.pallas_call(functools.partial(attend_gather_body, width), name='attend...  39.7 us
    dot_general x13, matrix products, dot_t(): lax.dot_general(left, right, (((1,), (1,)), ((), ())), preferred_element_...  37.9 us
    pallas_call x2, Pallas kernels, weight_grads(): pl.pallas_call(functools.partial(weight_grads_body, tuple(jobs), tuple(ta...  35.5 us
    pallas_call x2, Pallas kernels, exchange_all(): pl.pallas_call(exchange_body, name='exchange_all', out_shape=jax.ShapeDty...  31.7 us
    dot_general x13, matrix products, dot_float(): return jnp.dot(left, right, preferred_element_type=jnp.float32)  30.5 us
    pallas_call x2, Pallas kernels, attend_grads(): pl.pallas_call(functools.partial(attend_back_body, kind, width, scale), n...  30.4 us
  transfers between devices with their start and end apart: 5, of which 1 were waited for; matrix products, arithmetic and copies ran while one was open for 14% of the time, Pallas kernels for 53%

profile of v1, /device:TPU:0, one launch (start us, length us, event | category | flops | bytes accessed | tf_op | source)
XLA Modules:
  0.0 604.7 jit_solution(5642371510675745639)
XLA Ops:
  14.2 81.1 %gather_many.2 = (bf16[32,98,768]{2,1,0:T(8,128)(2,1)}, bf16[16,24,960]{2,1,0:T(8,128)(2,1)}, bf16[512,768]{1,0:T(8,128)(2,1)}, bf16[16,768]{1,0:T(8,128)(2,1)}) custom-call(bf16[98,768]{1,0:T(8,128)(2,1)} %bitcast.373, bf16[16,24,960]{2,1,0:T(8,128)(2,1)} %pad_maximum_fusion.3.refs_1_, bf16[512,768]{1,0:T(8,128)(2,1)} %bitcast.301, bf16[16,768]{1,0:T(8,128)(2,1)} %bitcast.375), custom_call_target="tpu_custom_call" | custom-call | tf_op jit(solution)/shard_map/gather_many/pallas_call | solution.py:274
  109.1 52.2 %gather_many.3 = bf16[3,32,8,3200]{3,2,1,0:T(8,128)(2,1)} custom-call(bf16[3,8,3200]{2,1,0:T(8,128)(2,1)} %copy-done.20), custom_call_target="tpu_custom_call" | custom-call | tf_op jit(solution)/shard_map/gather_many/pallas_call | solution.py:274
  161.3 4.6 stem_conv.2
  169.2 2.6 slice-done
  171.8 2.7 copy.226
  176.7 2.9 convolution_convert_fusion.1.refs_3_.k_ref
  179.7 3.2 convolution_convert_fusion.refs_4_.v_ref
  183.0 39.7 %attend_gather.1 = (bf16[512,768]{1,0:T(8,128)(2,1)S(1)}, f32[6,8,512]{2,1,0:T(8,128)S(1)}, bf16[3,32,8,3200]{3,2,1,0:T(8,128)(2,1)}) custom-call(s32[2]{0:T(128)S(1)} %pad_add_fusion.refs_0_.info_ref, f32[8,128]{1,0:T(8,128)S(1)} %broadcast_in_dim.22.refs_1_.ok_ref, bf16[512,768]{1,0:T(8,128)(2,1)S(1)} %fusion.29.refs_2_.q_ref, ...), custom_call_target="tpu_custom_call" | custom-call | tf_op jit(solution)/shard_map/attend_gather/pallas_call | solution.py:306
  222.8 5.4 stem_conv.3
  229.6 10.3 %exchange_all.2 = bf16[32,24,196]{2,1,0:T(8,128)(2,1)} custom-call(bf16[32,24,196]{2,1,0:T(8,128)(2,1)} %bitcast.335), custom_call_target="tpu_custom_call" | custom-call | tf_op jit(solution)/shard_map/exchange_all/pallas_call | solution.py:555
  250.8 6.7 %cross_attend.1 = (bf16[512,768]{1,0:T(8,128)(2,1)S(1)}, f32[6,8,512]{2,1,0:T(8,128)S(1)}) custom-call(s32[2]{0:T(128)S(1)} %pad_add_fusion.refs_0_.info_ref, f32[256,128]{1,0:T(8,128)S(1)} %broadcast_in_dim.24.ok_ref, bf16[512,768]{1,0:T(8,128)(2,1)S(1)} %fusion.30.q_ref, bf16[256,768]{1,0:T(8,128)(2,1)S(1)} %convolution_convert_fusion.7.k_ref, ...), custom_call_target="tpu_custom_call" | custom-call | flops 402653184 | bytes 2359296 | tf_op jit(solution)/shard_map/cross_attend/pallas_call | solution.py:1351
  271.4 7.2 %fusion.9.refs_3_ = bf16[512,3072]{1,0:T(8,128)(2,1)} fusion(bf16[3072,768]{1,0:T(8,128)(2,1)S(1)} %bitcast.312, f32[512,768]{1,0:T(8,128)S(1)} %fusion.41, f32[512,768]{1,0:T(8,128)S(1)} %fusion.40, f32[512,768]{1,0:T(8,128)S(1)} %fusion.38, f32[512,768]{1,0:T(8,128)S(1)} %fusion.36, bf16[1,512,768]{2,1,0:T(8,128)(2,1)S(1)} %copy-done.2), kind=kOutput, calls=%fused_computation.11 | convolution fusion | flops 2448949248 | bytes 14942208 | tf_op jit(solution)/shard_map/dot_general | solution.py:1491
  278.6 15.5 %weight_grads.2 = bf16[32,192,768]{2,1,0:T(8,128)(2,1)} custom-call(bf16[512,3072]{1,0:T(8,128)(2,1)S(1)} %multiply_convert_fusion.refs_0_, bf16[512,768]{1,0:T(8,128)(2,1)S(1)} %bitcast.285, bf16[512,768]{1,0:T(8,128)(2,1)S(1)} %add_convert_fusion.2.refs_2_, bf16[512,3072]{1,0:T(8,128)(2,1)} %fusion.9.refs_3_), custom_call_target="tpu_custom_call" | custom-call | flops 4831838208 | bytes 9437184 | tf_op jit(solution)/shard_map/weight_grads/pallas_call | solution.py:1465
  294.2 2.8 pad_maximum_fusion.2.refs_9_
  303.5 3.2 multiply_reduce_fusion
  307.6 2.6 convolution_convert_fusion.3.do_ref
  310.4 8.1 %cross_attend_back.1 = (bf16[512,768]{1,0:T(8,128)(2,1)S(1)}, bf16[256,768]{1,0:T(8,128)(2,1)S(1)}, bf16[256,768]{1,0:T(8,128)(2,1)S(1)}) custom-call(s32[2]{0:T(128)S(1)} %pad_add_fusion.refs_0_.info_ref, f32[256,128]{1,0:T(8,128)S(1)} %copy-done.22, bf16[512,768]{1,0:T(8,128)(2,1)S(1)} %copy-done.40, bf16[256,768]{1,0:T(8,128)(2,1)S(1)} %copy-done.42, ...), custom_call_target="tpu_custom_call" | custom-call | flops 1006632960 | bytes 4718592 | tf_op jit(solution)/shard_map/cross_attend_back/pallas_call | solution.py:1377
  318.6 3.2 multiply_reduce_fusion.1
  326.2 22.3 %self_attend_back.1 = (bf16[512,768]{1,0:T(8,128)(2,1)S(1)}, bf16[1024,768]{1,0:T(8,128)(2,1)S(1)}, bf16[1024,768]{1,0:T(8,128)(2,1)S(1)}) custom-call(s32[2]{0:T(128)S(1)} %pad_add_fusion.refs_0_.info_ref, f32[8,128]{1,0:T(8,128)S(1)} %broadcast_in_dim.22.refs_1_.ok_ref, bf16[512,768]{1,0:T(8,128)(2,1)S(1)} %copy-done.13, bf16[1024,768]{1,0:T(8,128)(2,1)} %copy-done.8, ...), custom_call_target="tpu_custom_call" | custom-call | flops 4026531840 | bytes 11796480 | tf_op jit(solution)/shard_map/self_attend_back/pallas_call | solution.py:1377
  351.8 20.0 %weight_grads.3 = bf16[32,192,768]{2,1,0:T(8,128)(2,1)} custom-call(bf16[512,768]{1,0:T(8,128)(2,1)S(1)} %get-tuple-element.69.refs_0_, bf16[512,768]{1,0:T(8,128)(2,1)S(1)} %fusion.42.refs_1_, bf16[512,768]{1,0:T(8,128)(2,1)S(1)} %add_convert_fusion.3.refs_2_, bf16[512,768]{1,0:T(8,128)(2,1)S(1)} %get-tuple-element.72.refs_3_, ...), custom_call_target="tpu_custom_call" | custom-call | flops 6039797760 | bytes 9437184 | tf_op jit(solution)/shard_map/weight_grads/pallas_call | solution.py:1465
  379.2 21.3 %exchange_all.3 = bf16[32,24,196]{2,1,0:T(8,128)(2,1)} custom-call(bf16[32,24,196]{2,1,0:T(8,128)(2,1)} %copy_bitcast_fusion.4.x_ref), custom_call_target="tpu_custom_call" | custom-call | tf_op jit(solution)/shard_map/exchange_all/pallas_call | solution.py:555
  403.9 7.6 %stem_conv_back.2 = (bf16[768,3200]{1,0:T(8,128)(2,1)}, bf16[216,768]{1,0:T(8,128)(2,1)S(1)}, f32[24,128]{1,0:T(8,128)S(1)}) custom-call(f32[24,3200]{1,0:T(8,128)S(1)} %pad.23.dy_ref, f32[24,3200]{1,0:T(8,128)S(1)} %copy-done.19, f32[24,128]{1,0:T(8,128)S(1)} %copy-done.26, f32[24,128]{1,0:T(8,128)S(1)} %pad.21.gb_ref, f32[16,3200]{1,0:T(8,128)S(1)} %copy-done.3, ...), custom_call_target="tpu_custom_call" | custom-call | tf_op jit(solution)/shard_map/stem_conv_back/pallas_call | solution.py:756
  413.8 37.8 %reduce_all.2 = f32[3,8,3200]{2,1,0:T(8,128)S(1)} custom-call(bf16[3,32,8,3200]{3,2,1,0:T(8,128)(2,1)S(1)} %bitcast.287), custom_call_target="tpu_custom_call" | custom-call | tf_op jit(solution)/shard_map/reduce_all/pallas_call | solution.py:479
  454.9 3.3 fusion.32
  458.2 2.9 convolution_add_fusion
  463.6 3.4 fusion.31
  467.0 3.5 fusion.28
  470.6 7.7 %stem_conv_back.3 = (bf16[768,3200]{1,0:T(8,128)(2,1)}, bf16[216,768]{1,0:T(8,128)(2,1)S(1)}, f32[24,128]{1,0:T(8,128)S(1)}) custom-call(f32[24,3200]{1,0:T(8,128)S(1)} %bitcast_add_fusion.1.dy_ref, f32[24,3200]{1,0:T(8,128)S(1)} %copy-done.17, f32[24,128]{1,0:T(8,128)S(1)} %copy-done.24, f32[24,128]{1,0:T(8,128)S(1)} %pad.21.gb_ref, ...), custom_call_target="tpu_custom_call" | custom-call | tf_op jit(solution)/shard_map/stem_conv_back/pallas_call | solution.py:756
  482.0 57.1 %reduce_all.3 = (f32[3,8,3200]{2,1,0:T(8,128)S(1)}, bf16[2,16,24,432]{3,2,1,0:T(8,128)(2,1)S(1)}, bf16[16,768]{1,0:T(8,128)(2,1)S(1)}) custom-call(bf16[3,32,8,3200]{3,2,1,0:T(8,128)(2,1)S(1)} %bitcast.286, bf16[16,24,432]{2,1,0:T(8,128)(2,1)S(1)} %bitcast.294, bf16[16,768]{1,0:T(8,128)(2,1)S(1)} %fusion.65.refs_2_), custom_call_target="tpu_custom_call" | custom-call | tf_op jit(solution)/shard_map/reduce_all/pallas_call | solution.py:479
  549.8 27.5 %swap_both.1 = (bf16[2,16,24,534]{3,2,1,0:T(8,128)(2,1)}, bf16[384,768]{1,0:T(8,128)(2,1)}) custom-call(bf16[16,24,534]{2,1,0:T(8,128)(2,1)} %fusion.58.x_ref, bf16[384,768]{1,0:T(8,128)(2,1)} %bitcast.326), custom_call_target="tpu_custom_call" | custom-call | tf_op jit(solution)/shard_map/swap_both/pallas_call | solution.py:508
  588.6 3.3 copy.260
  592.5 3.5 fusion.46
  (437 shorter events, 111.5 us)
Async XLA Ops:
  7.2 161.9 %all-gather.2.cloned.1.call-start = ((), (), s32[]{:S(2)}) async-start(), calls=%async_computation.2 | async-start | bytes 20054016 | tf_op jit(solution)/shard_map/all_gather | solution.py:1571
  9.8 460.8 %reduce-scatter.3.cloned.1.call-start = ((), (), s32[]{:S(2)}) async-start(), calls=%async_computation.3 | async-start | bytes 10027008 | tf_op jit(solution)/shard_map/reduce_scatter | solution.py:1673
  99.9 74.6 %copy-start.73 = (f32[768]{0:T(1024)}, f32[768]{0:T(1024)S(1)}, u32[]{:S(2)}) copy-start(f32[768]{0:T(1024)S(1)} %mul.297) | copy-start | bytes 9220
  100.0 144.1 %copy-start.87 = (f32[768]{0:T(1024)}, f32[768]{0:T(1024)S(1)}, u32[]{:S(2)}) copy-start(f32[768]{0:T(1024)S(1)} %mul.322) | copy-start | bytes 9220
  109.1 52.2 %copy-start.27 = (f32[24,128]{1,0:T(8,128)}, f32[24,128]{1,0:T(8,128)S(1)}, u32[]{:S(2)}) copy-start(f32[24,128]{1,0:T(8,128)S(1)} %get-tuple-element.94.rstd_ref) | copy-start | bytes 36868
  167.6 78.9 %copy-start.75 = (bf16[16,768]{1,0:T(8,128)(2,1)}, bf16[16,768]{1,0:T(8,128)(2,1)S(1)}, u32[]{:S(2)}) copy-start(bf16[16,768]{1,0:T(8,128)(2,1)S(1)} %get-tuple-element.208) | copy-start | bytes 73732
  167.6 78.9 %copy-start.77 = (bf16[16,768]{1,0:T(8,128)(2,1)}, bf16[16,768]{1,0:T(8,128)(2,1)S(1)}, u32[]{:S(2)}) copy-start(bf16[16,768]{1,0:T(8,128)(2,1)S(1)} %get-tuple-element.209) | copy-start | bytes 73732
  169.1 10.5 %copy-start.61 = (bf16[512,768]{1,0:T(8,128)(2,1)}, bf16[512,768]{1,0:T(8,128)(2,1)S(1)}, u32[]{:S(2)}) copy-start(bf16[512,768]{1,0:T(8,128)(2,1)S(1)} %get-tuple-element.211.refs_13_) | copy-start | bytes 2359300
  182.9 39.8 %copy-start.9 = (bf16[1024,768]{1,0:T(8,128)(2,1)}, bf16[1024,768]{1,0:T(8,128)(2,1)S(1)}, u32[]{:S(2)}) copy-start(bf16[1024,768]{1,0:T(8,128)(2,1)S(1)} %convolution_convert_fusion.refs_4_.v_ref) | copy-start | bytes 4718596
  228.2 12.9 %copy-start.18 = (f32[24,3200]{1,0:T(8,128)}, f32[24,3200]{1,0:T(8,128)S(1)}, u32[]{:S(2)}) copy-start(f32[24,3200]{1,0:T(8,128)S(1)} %get-tuple-element.79.n_ref) | copy-start | bytes 921604
  228.2 13.0 %copy-start.25 = (f32[24,128]{1,0:T(8,128)}, f32[24,128]{1,0:T(8,128)S(1)}, u32[]{:S(2)}) copy-start(f32[24,128]{1,0:T(8,128)S(1)} %get-tuple-element.80.rstd_ref) | copy-start | bytes 36868
  243.7 13.9 %copy-start.54 = (f32[512,768]{1,0:T(8,128)}, f32[512,768]{1,0:T(8,128)S(1)}, u32[]{:S(2)}) copy-start(f32[512,768]{1,0:T(8,128)S(1)} %get-tuple-element.213) | copy-start | bytes 4718596
  250.7 9.1 %copy-start.39 = (bf16[512,768]{1,0:T(8,128)(2,1)}, bf16[512,768]{1,0:T(8,128)(2,1)S(1)}, u32[]{:S(2)}) copy-start(bf16[512,768]{1,0:T(8,128)(2,1)S(1)} %fusion.30.q_ref) | copy-start | bytes 2359300
  250.8 9.0 %copy-start.21 = (f32[256,128]{1,0:T(8,128)}, f32[256,128]{1,0:T(8,128)S(1)}, u32[]{:S(2)}) copy-start(f32[256,128]{1,0:T(8,128)S(1)} %broadcast_in_dim.24.ok_ref) | copy-start | bytes 393220
  294.2 255.6 %reduce-scatter.5.cloned.1.call-start = ((), (), s32[]{:S(2)}) async-start(), calls=%async_computation.4 | async-start | bytes 10027008 | tf_op jit(solution)/shard_map/reduce_scatter | solution.py:1673
  307.3 15.2 %copy-start.53 = (f32[512,768]{1,0:T(8,128)}, f32[512,768]{1,0:T(8,128)S(1)}, u32[]{:S(2)}) copy-start(f32[512,768]{1,0:T(8,128)S(1)} %get-tuple-element.175) | copy-start | bytes 4718596
  307.3 15.2 %copy-start.96 = (f32[512]{0:T(512)}, f32[512]{0:T(512)S(1)}, u32[]{:S(2)}) copy-start(f32[512]{0:T(512)S(1)} %negate_multiply_fusion.2) | copy-start | bytes 6148
  310.4 8.2 %copy-start.55 = (f32[512,768]{1,0:T(8,128)S(1)}, f32[512,768]{1,0:T(8,128)}, u32[]{:S(2)}) copy-start(f32[512,768]{1,0:T(8,128)} %copy-done.54) | copy-start | bytes 4718596
  318.5 33.3 %copy-start.14 = (bf16[256,768]{1,0:T(8,128)(2,1)}, bf16[256,768]{1,0:T(8,128)(2,1)S(1)}, u32[]{:S(2)}) copy-start(bf16[256,768]{1,0:T(8,128)(2,1)S(1)} %get-tuple-element.78.refs_6_) | copy-start | bytes 1179652
  318.5 33.2 %copy-start.36 = (bf16[256,768]{1,0:T(8,128)(2,1)}, bf16[256,768]{1,0:T(8,128)(2,1)S(1)}, u32[]{:S(2)}) copy-start(bf16[256,768]{1,0:T(8,128)(2,1)S(1)} %get-tuple-element.77.refs_5_) | copy-start | bytes 1179652
  326.2 25.6 %copy-start.31 = (bf16[512,768]{1,0:T(8,128)(2,1)S(1)}, bf16[512,768]{1,0:T(8,128)(2,1)}, u32[]{:S(2)}) copy-start(bf16[512,768]{1,0:T(8,128)(2,1)} %copy-done.29) | copy-start | bytes 2359300
  377.9 85.6 %copy-start.70 = (f32[32,768]{1,0:T(8,128)}, f32[32,768]{1,0:T(8,128)S(1)}, u32[]{:S(2)}) copy-start(f32[32,768]{1,0:T(8,128)S(1)} %slice.370) | copy-start | bytes 294916
  454.9 12.1 %slice-start.3 = ((s8[4718592]{0:T(1024)(128)(4,1)}), s8[4194304]{0:T(1024)(128)(4,1)S(1)}, s32[]{:S(2)}) async-start(s8[4718592]{0:T(1024)(128)(4,1)} %bitcast.313), calls=%async_computation.8 | async-start | bytes 8388608
  458.2 8.8 %copy-start.49 = (f32[512,768]{1,0:T(8,128)S(1)}, f32[512,768]{1,0:T(8,128)}, u32[]{:S(2)}) copy-start(f32[512,768]{1,0:T(8,128)} %copy-done.47) | copy-start | bytes 4718596
  458.2 8.8 %slice-start.4 = ((s8[4718592]{0:T(1024)(128)(4,1)}), s8[524288]{0:T(1024)(128)(4,1)S(1)}, s32[]{:S(2)}) async-start(s8[4718592]{0:T(1024)(128)(4,1)} %bitcast.313), calls=%async_computation.9 | async-start | bytes 1048576
  462.1 77.2 %collective-permute-start = (bf16[512,768]{1,0:T(8,128)(2,1)}, bf16[512,768]{1,0:T(8,128)(2,1)}, u32[]{:S(2)}, u32[]{:S(2)}) collective-permute-start(bf16[512,768]{1,0:T(8,128)(2,1)} %slice.470), channel_id=1, source_target_pairs={{1,0},{3,2},{5,4},{7,6},{9,8},{11,10},{13,12},{15,14},{17,16},{19,... | collective-permute-start | bytes 2359304 | tf_op jit(solution)/shard_map/ppermute | solution.py:1697
  482.0 57.2 %copy-start.51 = (bf16[1,512,768]{2,1,0:T(8,128)(2,1)S(1)}, bf16[1,512,768]{2,1,0:T(8,128)(2,1)}, u32[]{:S(2)}) copy-start(bf16[1,512,768]{2,1,0:T(8,128)(2,1)} %param.17) | copy-start | bytes 2359300
  482.0 57.2 %copy-start.59 = (f32[1024,768]{1,0:T(8,128)S(1)}, f32[1024,768]{1,0:T(8,128)}, u32[]{:S(2)}) copy-start(f32[1024,768]{1,0:T(8,128)} %copy-done.58) | copy-start | bytes 9437188
  482.0 57.3 %copy-start.64 = (f32[512,768]{1,0:T(8,128)S(1)}, f32[512,768]{1,0:T(8,128)}, u32[]{:S(2)}) copy-start(f32[512,768]{1,0:T(8,128)} %fusion.31) | copy-start | bytes 4718596
  482.0 57.3 %copy-start.74 = (f32[768]{0:T(1024)S(1)}, f32[768]{0:T(1024)}, u32[]{:S(2)}) copy-start(f32[768]{0:T(1024)} %copy-done.73) | copy-start | bytes 9220
  482.0 57.3 %copy-start.82 = (f32[512]{0:T(512)S(1)}, f32[512]{0:T(512)}, u32[]{:S(2)}) copy-start(f32[512]{0:T(512)} %copy-done.81) | copy-start | bytes 6148
  580.4 15.7 %collective-permute-start.1 = (bf16[384,768]{1,0:T(8,128)(2,1)S(1)}, bf16[384,768]{1,0:T(8,128)(2,1)S(1)}, u32[]{:S(2)}, u32[]{:S(2)}) collective-permute-start(bf16[384,768]{1,0:T(8,128)(2,1)S(1)} %bitcast.356), channel_id=1, source_target_pairs={{0,1},{1,0},{2,3},{3,2},{4,5},{5,4},{6,7},{7,6},{8,9},{9,8},{10,11... | collective-permute-start | bytes 1769480 | tf_op jit(solution)/shard_map/ppermute | solution.py:1774
  (94 other events, 286.3 us)
Sparse Core Ops, SparseCore 0:
  10.2 152.3 all-gather.1
  294.3 122.9 reduce-scatter.2
  421.9 127.8 reduce-scatter.4

commit v2 on v1

--- a/solution.py
+++ b/solution.py
@@ -182,6 +182,11 @@
             recv_sem=pair_recv.at[j],
             device_id=(a, 1 - s),
             device_id_type=MESH,
+        )
+
+    def pair_own():
+        return pltpu.make_async_copy(
+            ins[count + swaps], outs[count + swaps], pair_send.at[pairs]
         )
 
     every = [(i, p) for i in range(count) for p in range(PORTIONS)]
@@ -213,8 +218,15 @@
             if k == 0:
                 for i, p in every:
                     own_copy(i, p).start()
-                for j in range(pairs):
+                for j in range(1, pairs):
                     pair_copy(j).start()
+                if pairs:
+
+                    @pl.when(s == 0)
+                    def _():
+                        pair_copy(0).start()
+                        pair_own().start()
+
                 if swaps:
                     swap_own().start()
                 for j in range(1, dp):
@@ -232,8 +244,19 @@
                 await_part(i, p, mask ^ 2)
         for j in range(1, dp):
             arrived(outs[count].at[lax.rem(a - j + dp, dp)], swap_recv.at[j])
-        for j in range(pairs):
+        for j in range(1, pairs):
             pair_copy(j).wait()
+        if pairs:
+
+            @pl.when(s == 0)
+            def _():
+                pair_copy(0).wait_send()
+                pair_own().wait()
+
+            @pl.when(s != 0)
+            def _():
+                arrived(outs[count + swaps], pair_recv.at[0])
+
         for i, p, mask, bit in sent:
             block(i, p, mask, bit).wait_send()
         for j in range(1, dp):
@@ -259,8 +282,8 @@
         pltpu.SemaphoreType.DMA((count, PORTIONS)),
         pltpu.SemaphoreType.DMA((16,)),
         pltpu.SemaphoreType.DMA((16,)),
-        pltpu.SemaphoreType.DMA((max(pairs, 1),)),
-        pltpu.SemaphoreType.DMA((max(pairs, 1),)),
+        pltpu.SemaphoreType.DMA((pairs + 1,)),
+        pltpu.SemaphoreType.DMA((pairs + 1,)),
     ]
 
 

time: 615 us -> 615 us (level)
  no operation moved by 1% of the time
where the time goes in v2:
time: 615 us; the launch traced here: 605 us
  Pallas kernels  431 us (70%)
  matrix products  68.4 us (11%)
  local copies, waits for them, and re-layouts  55.1 us (9%)
  other arithmetic  28 us (5%)
  between operations  17.9 us (3%)
    pallas_call x2, Pallas kernels, gather_many(): pl.pallas_call(functools.partial(gather_body, tuple(kinds), len(swaps), l...  133 us
    pallas_call x2, Pallas kernels, reduce_all(): pl.pallas_call(functools.partial(reduce_body, len(swaps)), name='reduce_a...  94.8 us
    pallas_call x1, Pallas kernels, attend_gather(): pl.pallas_call(functools.partial(attend_gather_body, width), name='attend...  39.8 us
    dot_general x13, matrix products, dot_t(): lax.dot_general(left, right, (((1,), (1,)), ((), ())), preferred_element_...  37.9 us
    pallas_call x2, Pallas kernels, weight_grads(): pl.pallas_call(functools.partial(weight_grads_body, tuple(jobs), tuple(ta...  35.5 us
    pallas_call x2, Pallas kernels, exchange_all(): pl.pallas_call(exchange_body, name='exchange_all', out_shape=jax.ShapeDty...  31.7 us
    dot_general x13, matrix products, dot_float(): return jnp.dot(left, right, preferred_element_type=jnp.float32)  30.5 us
    pallas_call x2, Pallas kernels, attend_grads(): pl.pallas_call(functools.partial(attend_back_body, kind, width, scale), n...  30.4 us
  transfers between devices with their start and end apart: 5, of which 1 were waited for; matrix products, arithmetic and copies ran while one was open for 14% of the time, Pallas kernels for 53%

profile of v2, /device:TPU:0, one launch (start us, length us, event | category | flops | bytes accessed | tf_op | source)
XLA Modules:
  0.0 605.0 jit_solution(12597561730897566113)
XLA Ops:
  14.2 81.1 %gather_many.2 = (bf16[32,98,768]{2,1,0:T(8,128)(2,1)}, bf16[16,24,960]{2,1,0:T(8,128)(2,1)}, bf16[512,768]{1,0:T(8,128)(2,1)}, bf16[16,768]{1,0:T(8,128)(2,1)}) custom-call(bf16[98,768]{1,0:T(8,128)(2,1)} %bitcast.373, bf16[16,24,960]{2,1,0:T(8,128)(2,1)} %pad_maximum_fusion.3.refs_1_, bf16[512,768]{1,0:T(8,128)(2,1)} %bitcast.301, bf16[16,768]{1,0:T(8,128)(2,1)} %bitcast.375), custom_call_target="tpu_custom_call" | custom-call | tf_op jit(solution)/shard_map/gather_many/pallas_call | solution.py:297
  109.1 52.2 %gather_many.3 = bf16[3,32,8,3200]{3,2,1,0:T(8,128)(2,1)} custom-call(bf16[3,8,3200]{2,1,0:T(8,128)(2,1)} %copy-done.20), custom_call_target="tpu_custom_call" | custom-call | tf_op jit(solution)/shard_map/gather_many/pallas_call | solution.py:297
  161.3 4.6 stem_conv.2
  169.2 2.6 slice-done
  171.8 2.7 copy.226
  176.8 2.9 convolution_convert_fusion.1.refs_3_.k_ref
  179.7 3.2 convolution_convert_fusion.refs_4_.v_ref
  183.0 39.8 %attend_gather.1 = (bf16[512,768]{1,0:T(8,128)(2,1)S(1)}, f32[6,8,512]{2,1,0:T(8,128)S(1)}, bf16[3,32,8,3200]{3,2,1,0:T(8,128)(2,1)}) custom-call(s32[2]{0:T(128)S(1)} %pad_add_fusion.refs_0_.info_ref, f32[8,128]{1,0:T(8,128)S(1)} %broadcast_in_dim.22.refs_1_.ok_ref, bf16[512,768]{1,0:T(8,128)(2,1)S(1)} %fusion.29.refs_2_.q_ref, ...), custom_call_target="tpu_custom_call" | custom-call | tf_op jit(solution)/shard_map/attend_gather/pallas_call | solution.py:329
  222.9 5.4 stem_conv.3
  229.8 10.4 %exchange_all.2 = bf16[32,24,196]{2,1,0:T(8,128)(2,1)} custom-call(bf16[32,24,196]{2,1,0:T(8,128)(2,1)} %bitcast.335), custom_call_target="tpu_custom_call" | custom-call | tf_op jit(solution)/shard_map/exchange_all/pallas_call | solution.py:578
  251.0 6.7 %cross_attend.1 = (bf16[512,768]{1,0:T(8,128)(2,1)S(1)}, f32[6,8,512]{2,1,0:T(8,128)S(1)}) custom-call(s32[2]{0:T(128)S(1)} %pad_add_fusion.refs_0_.info_ref, f32[256,128]{1,0:T(8,128)S(1)} %broadcast_in_dim.24.ok_ref, bf16[512,768]{1,0:T(8,128)(2,1)S(1)} %fusion.30.q_ref, bf16[256,768]{1,0:T(8,128)(2,1)S(1)} %convolution_convert_fusion.7.k_ref, ...), custom_call_target="tpu_custom_call" | custom-call | flops 402653184 | bytes 2359296 | tf_op jit(solution)/shard_map/cross_attend/pallas_call | solution.py:1374
  271.5 7.2 %fusion.9.refs_3_ = bf16[512,3072]{1,0:T(8,128)(2,1)} fusion(bf16[3072,768]{1,0:T(8,128)(2,1)S(1)} %bitcast.312, f32[512,768]{1,0:T(8,128)S(1)} %fusion.41, f32[512,768]{1,0:T(8,128)S(1)} %fusion.40, f32[512,768]{1,0:T(8,128)S(1)} %fusion.38, f32[512,768]{1,0:T(8,128)S(1)} %fusion.36, bf16[1,512,768]{2,1,0:T(8,128)(2,1)S(1)} %copy-done.2), kind=kOutput, calls=%fused_computation.11 | convolution fusion | flops 2448949248 | bytes 14942208 | tf_op jit(solution)/shard_map/dot_general | solution.py:1514
  278.7 15.5 %weight_grads.2 = bf16[32,192,768]{2,1,0:T(8,128)(2,1)} custom-call(bf16[512,3072]{1,0:T(8,128)(2,1)S(1)} %multiply_convert_fusion.refs_0_, bf16[512,768]{1,0:T(8,128)(2,1)S(1)} %bitcast.285, bf16[512,768]{1,0:T(8,128)(2,1)S(1)} %add_convert_fusion.2.refs_2_, bf16[512,3072]{1,0:T(8,128)(2,1)} %fusion.9.refs_3_), custom_call_target="tpu_custom_call" | custom-call | flops 4831838208 | bytes 9437184 | tf_op jit(solution)/shard_map/weight_grads/pallas_call | solution.py:1488
  294.4 2.8 pad_maximum_fusion.2.refs_9_
  303.6 3.2 multiply_reduce_fusion
  307.8 2.6 convolution_convert_fusion.3.do_ref
  310.5 8.1 %cross_attend_back.1 = (bf16[512,768]{1,0:T(8,128)(2,1)S(1)}, bf16[256,768]{1,0:T(8,128)(2,1)S(1)}, bf16[256,768]{1,0:T(8,128)(2,1)S(1)}) custom-call(s32[2]{0:T(128)S(1)} %pad_add_fusion.refs_0_.info_ref, f32[256,128]{1,0:T(8,128)S(1)} %copy-done.22, bf16[512,768]{1,0:T(8,128)(2,1)S(1)} %copy-done.40, bf16[256,768]{1,0:T(8,128)(2,1)S(1)} %copy-done.42, ...), custom_call_target="tpu_custom_call" | custom-call | flops 1006632960 | bytes 4718592 | tf_op jit(solution)/shard_map/cross_attend_back/pallas_call | solution.py:1400
  318.7 3.2 multiply_reduce_fusion.1
  326.4 22.3 %self_attend_back.1 = (bf16[512,768]{1,0:T(8,128)(2,1)S(1)}, bf16[1024,768]{1,0:T(8,128)(2,1)S(1)}, bf16[1024,768]{1,0:T(8,128)(2,1)S(1)}) custom-call(s32[2]{0:T(128)S(1)} %pad_add_fusion.refs_0_.info_ref, f32[8,128]{1,0:T(8,128)S(1)} %broadcast_in_dim.22.refs_1_.ok_ref, bf16[512,768]{1,0:T(8,128)(2,1)S(1)} %copy-done.13, bf16[1024,768]{1,0:T(8,128)(2,1)} %copy-done.8, ...), custom_call_target="tpu_custom_call" | custom-call | flops 4026531840 | bytes 11796480 | tf_op jit(solution)/shard_map/self_attend_back/pallas_call | solution.py:1400
  351.9 20.0 %weight_grads.3 = bf16[32,192,768]{2,1,0:T(8,128)(2,1)} custom-call(bf16[512,768]{1,0:T(8,128)(2,1)S(1)} %get-tuple-element.69.refs_0_, bf16[512,768]{1,0:T(8,128)(2,1)S(1)} %fusion.42.refs_1_, bf16[512,768]{1,0:T(8,128)(2,1)S(1)} %add_convert_fusion.3.refs_2_, bf16[512,768]{1,0:T(8,128)(2,1)S(1)} %get-tuple-element.72.refs_3_, ...), custom_call_target="tpu_custom_call" | custom-call | flops 6039797760 | bytes 9437184 | tf_op jit(solution)/shard_map/weight_grads/pallas_call | solution.py:1488
  379.3 21.3 %exchange_all.3 = bf16[32,24,196]{2,1,0:T(8,128)(2,1)} custom-call(bf16[32,24,196]{2,1,0:T(8,128)(2,1)} %copy_bitcast_fusion.4.x_ref), custom_call_target="tpu_custom_call" | custom-call | tf_op jit(solution)/shard_map/exchange_all/pallas_call | solution.py:578
  404.0 7.6 %stem_conv_back.2 = (bf16[768,3200]{1,0:T(8,128)(2,1)}, bf16[216,768]{1,0:T(8,128)(2,1)S(1)}, f32[24,128]{1,0:T(8,128)S(1)}) custom-call(f32[24,3200]{1,0:T(8,128)S(1)} %pad.23.dy_ref, f32[24,3200]{1,0:T(8,128)S(1)} %copy-done.19, f32[24,128]{1,0:T(8,128)S(1)} %copy-done.26, f32[24,128]{1,0:T(8,128)S(1)} %pad.21.gb_ref, f32[16,3200]{1,0:T(8,128)S(1)} %copy-done.3, ...), custom_call_target="tpu_custom_call" | custom-call | tf_op jit(solution)/shard_map/stem_conv_back/pallas_call | solution.py:779
  414.0 38.0 %reduce_all.2 = f32[3,8,3200]{2,1,0:T(8,128)S(1)} custom-call(bf16[3,32,8,3200]{3,2,1,0:T(8,128)(2,1)S(1)} %bitcast.287), custom_call_target="tpu_custom_call" | custom-call | tf_op jit(solution)/shard_map/reduce_all/pallas_call | solution.py:502
  455.2 3.3 fusion.32
  458.6 2.9 convolution_add_fusion
  464.0 3.4 fusion.31
  467.4 3.5 fusion.28
  471.0 7.7 %stem_conv_back.3 = (bf16[768,3200]{1,0:T(8,128)(2,1)}, bf16[216,768]{1,0:T(8,128)(2,1)S(1)}, f32[24,128]{1,0:T(8,128)S(1)}) custom-call(f32[24,3200]{1,0:T(8,128)S(1)} %bitcast_add_fusion.1.dy_ref, f32[24,3200]{1,0:T(8,128)S(1)} %copy-done.17, f32[24,128]{1,0:T(8,128)S(1)} %copy-done.24, f32[24,128]{1,0:T(8,128)S(1)} %pad.21.gb_ref, ...), custom_call_target="tpu_custom_call" | custom-call | tf_op jit(solution)/shard_map/stem_conv_back/pallas_call | solution.py:779
  482.4 56.8 %reduce_all.3 = (f32[3,8,3200]{2,1,0:T(8,128)S(1)}, bf16[2,16,24,432]{3,2,1,0:T(8,128)(2,1)S(1)}, bf16[16,768]{1,0:T(8,128)(2,1)S(1)}) custom-call(bf16[3,32,8,3200]{3,2,1,0:T(8,128)(2,1)S(1)} %bitcast.286, bf16[16,24,432]{2,1,0:T(8,128)(2,1)S(1)} %bitcast.294, bf16[16,768]{1,0:T(8,128)(2,1)S(1)} %fusion.65.refs_2_), custom_call_target="tpu_custom_call" | custom-call | tf_op jit(solution)/shard_map/reduce_all/pallas_call | solution.py:502
  549.9 27.3 %swap_both.1 = (bf16[2,16,24,534]{3,2,1,0:T(8,128)(2,1)}, bf16[384,768]{1,0:T(8,128)(2,1)}) custom-call(bf16[16,24,534]{2,1,0:T(8,128)(2,1)} %fusion.58.x_ref, bf16[384,768]{1,0:T(8,128)(2,1)} %bitcast.326), custom_call_target="tpu_custom_call" | custom-call | tf_op jit(solution)/shard_map/swap_both/pallas_call | solution.py:531
  588.8 3.3 copy.260
  592.8 3.5 fusion.46
  (437 shorter events, 111.9 us)
Async XLA Ops:
  7.2 162.0 %all-gather.2.cloned.1.call-start = ((), (), s32[]{:S(2)}) async-start(), calls=%async_computation.2 | async-start | bytes 20054016 | tf_op jit(solution)/shard_map/all_gather | solution.py:1594
  9.8 461.2 %reduce-scatter.3.cloned.1.call-start = ((), (), s32[]{:S(2)}) async-start(), calls=%async_computation.3 | async-start | bytes 10027008 | tf_op jit(solution)/shard_map/reduce_scatter | solution.py:1696
  99.9 74.6 %copy-start.73 = (f32[768]{0:T(1024)}, f32[768]{0:T(1024)S(1)}, u32[]{:S(2)}) copy-start(f32[768]{0:T(1024)S(1)} %mul.297) | copy-start | bytes 9220
  100.0 144.3 %copy-start.87 = (f32[768]{0:T(1024)}, f32[768]{0:T(1024)S(1)}, u32[]{:S(2)}) copy-start(f32[768]{0:T(1024)S(1)} %mul.322) | copy-start | bytes 9220
  109.1 52.2 %copy-start.27 = (f32[24,128]{1,0:T(8,128)}, f32[24,128]{1,0:T(8,128)S(1)}, u32[]{:S(2)}) copy-start(f32[24,128]{1,0:T(8,128)S(1)} %get-tuple-element.94.rstd_ref) | copy-start | bytes 36868
  167.7 79.0 %copy-start.75 = (bf16[16,768]{1,0:T(8,128)(2,1)}, bf16[16,768]{1,0:T(8,128)(2,1)S(1)}, u32[]{:S(2)}) copy-start(bf16[16,768]{1,0:T(8,128)(2,1)S(1)} %get-tuple-element.208) | copy-start | bytes 73732
  167.7 79.0 %copy-start.77 = (bf16[16,768]{1,0:T(8,128)(2,1)}, bf16[16,768]{1,0:T(8,128)(2,1)S(1)}, u32[]{:S(2)}) copy-start(bf16[16,768]{1,0:T(8,128)(2,1)S(1)} %get-tuple-element.209) | copy-start | bytes 73732
  169.2 10.5 %copy-start.61 = (bf16[512,768]{1,0:T(8,128)(2,1)}, bf16[512,768]{1,0:T(8,128)(2,1)S(1)}, u32[]{:S(2)}) copy-start(bf16[512,768]{1,0:T(8,128)(2,1)S(1)} %get-tuple-element.211.refs_13_) | copy-start | bytes 2359300
  183.0 39.9 %copy-start.9 = (bf16[1024,768]{1,0:T(8,128)(2,1)}, bf16[1024,768]{1,0:T(8,128)(2,1)S(1)}, u32[]{:S(2)}) copy-start(bf16[1024,768]{1,0:T(8,128)(2,1)S(1)} %convolution_convert_fusion.refs_4_.v_ref) | copy-start | bytes 4718596
  228.4 12.9 %copy-start.18 = (f32[24,3200]{1,0:T(8,128)}, f32[24,3200]{1,0:T(8,128)S(1)}, u32[]{:S(2)}) copy-start(f32[24,3200]{1,0:T(8,128)S(1)} %get-tuple-element.79.n_ref) | copy-start | bytes 921604
  228.4 13.0 %copy-start.25 = (f32[24,128]{1,0:T(8,128)}, f32[24,128]{1,0:T(8,128)S(1)}, u32[]{:S(2)}) copy-start(f32[24,128]{1,0:T(8,128)S(1)} %get-tuple-element.80.rstd_ref) | copy-start | bytes 36868
  243.9 13.9 %copy-start.54 = (f32[512,768]{1,0:T(8,128)}, f32[512,768]{1,0:T(8,128)S(1)}, u32[]{:S(2)}) copy-start(f32[512,768]{1,0:T(8,128)S(1)} %get-tuple-element.213) | copy-start | bytes 4718596
  250.8 9.1 %copy-start.39 = (bf16[512,768]{1,0:T(8,128)(2,1)}, bf16[512,768]{1,0:T(8,128)(2,1)S(1)}, u32[]{:S(2)}) copy-start(bf16[512,768]{1,0:T(8,128)(2,1)S(1)} %fusion.30.q_ref) | copy-start | bytes 2359300
  251.0 8.9 %copy-start.21 = (f32[256,128]{1,0:T(8,128)}, f32[256,128]{1,0:T(8,128)S(1)}, u32[]{:S(2)}) copy-start(f32[256,128]{1,0:T(8,128)S(1)} %broadcast_in_dim.24.ok_ref) | copy-start | bytes 393220
  294.3 255.6 %reduce-scatter.5.cloned.1.call-start = ((), (), s32[]{:S(2)}) async-start(), calls=%async_computation.4 | async-start | bytes 10027008 | tf_op jit(solution)/shard_map/reduce_scatter | solution.py:1696
  307.4 15.2 %copy-start.53 = (f32[512,768]{1,0:T(8,128)}, f32[512,768]{1,0:T(8,128)S(1)}, u32[]{:S(2)}) copy-start(f32[512,768]{1,0:T(8,128)S(1)} %get-tuple-element.175) | copy-start | bytes 4718596
  307.4 15.2 %copy-start.96 = (f32[512]{0:T(512)}, f32[512]{0:T(512)S(1)}, u32[]{:S(2)}) copy-start(f32[512]{0:T(512)S(1)} %negate_multiply_fusion.2) | copy-start | bytes 6148
  310.5 8.2 %copy-start.55 = (f32[512,768]{1,0:T(8,128)S(1)}, f32[512,768]{1,0:T(8,128)}, u32[]{:S(2)}) copy-start(f32[512,768]{1,0:T(8,128)} %copy-done.54) | copy-start | bytes 4718596
  318.6 33.3 %copy-start.14 = (bf16[256,768]{1,0:T(8,128)(2,1)}, bf16[256,768]{1,0:T(8,128)(2,1)S(1)}, u32[]{:S(2)}) copy-start(bf16[256,768]{1,0:T(8,128)(2,1)S(1)} %get-tuple-element.78.refs_6_) | copy-start | bytes 1179652
  318.6 33.3 %copy-start.36 = (bf16[256,768]{1,0:T(8,128)(2,1)}, bf16[256,768]{1,0:T(8,128)(2,1)S(1)}, u32[]{:S(2)}) copy-start(bf16[256,768]{1,0:T(8,128)(2,1)S(1)} %get-tuple-element.77.refs_5_) | copy-start | bytes 1179652
  326.3 25.6 %copy-start.31 = (bf16[512,768]{1,0:T(8,128)(2,1)S(1)}, bf16[512,768]{1,0:T(8,128)(2,1)}, u32[]{:S(2)}) copy-start(bf16[512,768]{1,0:T(8,128)(2,1)} %copy-done.29) | copy-start | bytes 2359300
  378.0 85.9 %copy-start.70 = (f32[32,768]{1,0:T(8,128)}, f32[32,768]{1,0:T(8,128)S(1)}, u32[]{:S(2)}) copy-start(f32[32,768]{1,0:T(8,128)S(1)} %slice.370) | copy-start | bytes 294916
  455.2 12.1 %slice-start.3 = ((s8[4718592]{0:T(1024)(128)(4,1)}), s8[4194304]{0:T(1024)(128)(4,1)S(1)}, s32[]{:S(2)}) async-start(s8[4718592]{0:T(1024)(128)(4,1)} %bitcast.313), calls=%async_computation.8 | async-start | bytes 8388608
  458.6 8.8 %copy-start.49 = (f32[512,768]{1,0:T(8,128)S(1)}, f32[512,768]{1,0:T(8,128)}, u32[]{:S(2)}) copy-start(f32[512,768]{1,0:T(8,128)} %copy-done.47) | copy-start | bytes 4718596
  458.6 8.8 %slice-start.4 = ((s8[4718592]{0:T(1024)(128)(4,1)}), s8[524288]{0:T(1024)(128)(4,1)S(1)}, s32[]{:S(2)}) async-start(s8[4718592]{0:T(1024)(128)(4,1)} %bitcast.313), calls=%async_computation.9 | async-start | bytes 1048576
  462.4 76.9 %collective-permute-start = (bf16[512,768]{1,0:T(8,128)(2,1)}, bf16[512,768]{1,0:T(8,128)(2,1)}, u32[]{:S(2)}, u32[]{:S(2)}) collective-permute-start(bf16[512,768]{1,0:T(8,128)(2,1)} %slice.470), channel_id=1, source_target_pairs={{1,0},{3,2},{5,4},{7,6},{9,8},{11,10},{13,12},{15,14},{17,16},{19,... | collective-permute-start | bytes 2359304 | tf_op jit(solution)/shard_map/ppermute | solution.py:1720
  482.4 56.9 %copy-start.51 = (bf16[1,512,768]{2,1,0:T(8,128)(2,1)S(1)}, bf16[1,512,768]{2,1,0:T(8,128)(2,1)}, u32[]{:S(2)}) copy-start(bf16[1,512,768]{2,1,0:T(8,128)(2,1)} %param.17) | copy-start | bytes 2359300
  482.4 56.9 %copy-start.59 = (f32[1024,768]{1,0:T(8,128)S(1)}, f32[1024,768]{1,0:T(8,128)}, u32[]{:S(2)}) copy-start(f32[1024,768]{1,0:T(8,128)} %copy-done.58) | copy-start | bytes 9437188
  482.4 56.9 %copy-start.64 = (f32[512,768]{1,0:T(8,128)S(1)}, f32[512,768]{1,0:T(8,128)}, u32[]{:S(2)}) copy-start(f32[512,768]{1,0:T(8,128)} %fusion.31) | copy-start | bytes 4718596
  482.4 56.9 %copy-start.74 = (f32[768]{0:T(1024)S(1)}, f32[768]{0:T(1024)}, u32[]{:S(2)}) copy-start(f32[768]{0:T(1024)} %copy-done.73) | copy-start | bytes 9220
  482.4 56.9 %copy-start.82 = (f32[512]{0:T(512)S(1)}, f32[512]{0:T(512)}, u32[]{:S(2)}) copy-start(f32[512]{0:T(512)} %copy-done.81) | copy-start | bytes 6148
  580.2 16.1 %collective-permute-start.1 = (bf16[384,768]{1,0:T(8,128)(2,1)S(1)}, bf16[384,768]{1,0:T(8,128)(2,1)S(1)}, u32[]{:S(2)}, u32[]{:S(2)}) collective-permute-start(bf16[384,768]{1,0:T(8,128)(2,1)S(1)} %bitcast.356), channel_id=1, source_target_pairs={{0,1},{1,0},{2,3},{3,2},{4,5},{5,4},{6,7},{7,6},{8,9},{9,8},{10,11... | collective-permute-start | bytes 1769480 | tf_op jit(solution)/shard_map/ppermute | solution.py:1797
  (94 other events, 286.2 us)
Sparse Core Ops, SparseCore 0:
  10.2 152.3 all-gather.1
  294.4 122.9 reduce-scatter.2
  422.1 127.7 reduce-scatter.4
